TPU v7x, 128 devices: a whole 4x4x4 slice. The times are simulated.
128 devices in a mesh: sfc: 128 (over y, z, x, core).
Axes of the slice: x: 4, y: 4, z: 4, core: 2. Of those that a mesh axis runs over, the one named last changes fastest.
Arguments:
- tracers: float32 [8192, 3, 480], P('sfc'), may hold values from -6 to 6
- weights: float32 [2, 8192, 3, 256], P(None, 'sfc'), may hold values from -1.5 to 1.5
- departure: int32 [8192, 48], P('sfc'), may hold values from 0 to 95, as said below
- needs: int32 [128, 8, 4], P('sfc'), may hold values from 0 to 63
- counts: int32 [128, 8], P('sfc'), may hold values from 1 to 4, as said below
Outputs:
- mixed: float32 [8192, 3, 480], P('sfc')
Inputs may be any that keep to these rules, and one draw needn't show every extreme that they name: `departure`: each entry is a slot of its range's source table: below 64 a local element; otherwise 64 + j * 4 + c with c below counts[r, j] of its range r. `counts`: some range uses all 4 entries of every list in every draw.
All inputs are finite; a program needn't handle non-finite values.
Results may differ from a plain program's by a relative error of at most 0.0003.
Values sent between devices are 32-bit elements; how exact they have to be, the bound alone decides.
No kernel may reach another device: no remote copies, remote signals or barrier semaphores. Data moves between devices by JAX's collectives and lax.ppermute only.
A program may use at most 64 MiB of HBM per device.

v0:
```python
import jax
import jax.numpy as jnp
from jax import lax
from jax.experimental import pallas as pl
from jax.experimental.pallas import tpu as pltpu
from jax.sharding import PartitionSpec as P


NODES = 16
TRACERS = 30
LEV = 3
SUBSTEPS = 2
REACH = 4
CAP = 4
ELEMS = 64
ROW = NODES * TRACERS
WIDE = 32
TALL = NODES * WIDE
REMOTE = 2 * REACH * CAP
DEPTH = 2 * ELEMS + 2 * REMOTE
PAIRS = 4
LANES = 128
N = 128


VMEM = pl.BlockSpec(memory_space=pltpu.VMEM)
HBM = pl.BlockSpec(memory_space=pltpu.HBM)
SMEM = pl.BlockSpec(memory_space=pltpu.SMEM)
f32 = jnp.float32
bf16 = jnp.bfloat16


def moved(value, target):
    return lax.ppermute(value, "sfc", [(source, target(source) % N) for source in range(N)])


def swapped(value):
    return moved(value, lambda device: device ^ 1)


def ahead(value, chips):
    return moved(value, lambda device: device + 2 * chips * (1 - 2 * (device % 2)))


def split(x):
    high = x.astype(bf16).astype(f32)
    return high, x - high


def prepare(me, counts_in, tracers_in, weights_in, departure_in, table, hot, turned, tracers,
            spaced, counts, weights, departure, done):
    copies = [pltpu.make_async_copy(source, target, done.at[i]) for i, (source, target) in enumerate(
        [(tracers_in, tracers), (counts_in, counts), (departure_in, departure), (weights_in, weights)])]
    for copy in copies:
        copy.start()
    spaced[ROW:, :] = jnp.zeros_like(spaced[ROW:, :])
    copies[0].wait()
    copies[1].wait()
    copies[2].wait()
    slot = lax.broadcasted_iota(jnp.int32, (REMOTE, LANES), 0)
    group, entry = slot // CAP, slot % CAP
    limit = base = jnp.zeros_like(slot)
    for q in range(2 * REACH):
        j = jnp.where(me[0] == 0, HELD[0][q], HELD[1][q])
        limit = jnp.where(group == q, counts[0, j], limit)
        base = jnp.where(group == q, ELEMS + j * CAP, base)
    far_slot = jnp.where(entry < limit, base + entry, -1)
    near_slot = lax.broadcasted_iota(jnp.int32, (ELEMS, LANES), 0)
    for level in range(LEV):
        high, low = split(tracers[level])
        spaced[0:ROW, :] = jnp.concatenate([high, low], axis=0).T
        for k in range(NODES):
            table[level, k * WIDE:(k + 1) * WIDE, :] = spaced[k * TRACERS:k * TRACERS + WIDE, :].astype(bf16)
        upper = departure[level * NODES:level * NODES + 8, :]
        lower = departure[level * NODES + 8:level * NODES + 16, :]
        wanted = jnp.concatenate([upper, lower], axis=1)
        for t in range(8):
            row = wanted[t:t + 1, :]
            near = (near_slot == row).astype(f32).astype(bf16)
            far = (far_slot == row).astype(f32).astype(bf16)
            lanes = slice((t % 2) * LANES, (t % 2 + 1) * LANES)
            hot[level, t // 2, :, lanes] = jnp.concatenate([near, near, far, far], axis=0)
    copies[3].wait()
    for level in range(LEV):
        for step in range(SUBSTEPS):
            both = jnp.concatenate([weights[step, level, :, 0:LANES], weights[step, level, :, LANES:2 * LANES]], axis=0)
            turned[step, level] = both.T


def pack(width, me, asked2, asked1, lists, own, other, near, far, inner):
    lane = lax.broadcasted_iota(jnp.int32, (CAP, LANES), 1)
    sources = [asked1.at[0], asked1.at[1], asked2.at[0], asked2.at[1], lists]
    picks = []
    for source, first, second in PACKED:
        one = [sources[source][:, j:j + 1] + ELEMS * place for j, place in (first, second)]
        picks.append((jnp.broadcast_to(jnp.where(me[0] == 0, one[0], one[1]), (CAP, LANES)) == lane).astype(f32))
    picks = jnp.concatenate(picks, axis=0).astype(bf16)
    picks = jnp.concatenate([picks, picks, picks], axis=1)

    def give(level, lanes, rows):
        near[0, level, :, lanes] = rows[0:8]
        near[1, level, :, lanes] = rows[8:16]
        for g in range(3):
            far[g, level, :, lanes] = rows[16 + 4 * g:20 + 4 * g]
        inner[level, :, lanes] = rows[28:32]

    for level in range(LEV):
        both = jnp.concatenate([own[level], other[level]], axis=0)
        high, rest = split(both)
        middle, low = split(rest)
        parts = jnp.concatenate([high.astype(bf16), middle.astype(bf16), low.astype(bf16)], axis=0)
        rows = jnp.dot(picks, parts, preferred_element_type=f32)
        if width == TALL:
            give(level, slice(0, TALL), rows)
        else:
            spread = []
            for k in range(NODES):
                spread += [rows[:, k * TRACERS:(k + 1) * TRACERS], jnp.zeros((REMOTE, WIDE - TRACERS), f32)]
            give(level, slice(0, TALL), jnp.concatenate(spread, axis=1))


def substep(step, near, far, near_other, far_other, inner, table, hot, turned, out, whole, mixed, close):
    last = step + 1 == SUBSTEPS
    for level in range(LEV):
        rows = jnp.concatenate(
            [near[0, level], far[0, level], near_other[1, level], far_other[1, level], far_other[2, level], inner[level]],
            axis=0)
        high, low = split(rows)
        whole[level, :, 0:2 * ELEMS] = table[level]
        whole[level, :, 2 * ELEMS:] = jnp.concatenate([high, low], axis=0).T.astype(bf16)

    for level in range(LEV):
        for pair in range(PAIRS):
            gathered = jnp.dot(whole[level], hot[level, pair], preferred_element_type=f32)
            for half in range(2):
                lanes = slice(half * LANES, (half + 1) * LANES)
                t = pair * 2 + half
                factors = turned[step, level, t * NODES:(t + 1) * NODES, :]
                total = lowest = highest = None
                for k in range(NODES):
                    piece = gathered[k * WIDE:(k + 1) * WIDE, lanes]
                    term = piece * factors[k:k + 1, :]
                    total = term if k == 0 else total + term
                    lowest = piece if k == 0 else jnp.minimum(lowest, piece)
                    highest = piece if k == 0 else jnp.maximum(highest, piece)
                result = jnp.minimum(jnp.maximum(total, lowest), highest)
                if last:
                    close[level, t * TRACERS:(t + 1) * TRACERS, :] = result[:TRACERS]
                else:
                    mixed[level, t * WIDE:(t + 1) * WIDE, :] = result
        if last:
            rows = close[level].T
            half = 8 * TRACERS
            out[level, :, 0:half] = rows[:ELEMS, 0:half]
            out[level, :, half:2 * half] = rows[ELEMS:, 0:half]
        else:
            rows = mixed[level].T
            out[level, :, 0:8 * WIDE] = rows[:ELEMS]
            out[level, :, 8 * WIDE:] = rows[ELEMS:]


def retable(tracers, table):
    for level in range(LEV):
        high, low = split(tracers[level])
        table[level] = jnp.concatenate([high, low], axis=0).T.astype(bf16)


def shaped(*dims, dtype=f32):
    return jax.ShapeDtypeStruct(dims, dtype)


TABLE = shaped(LEV, TALL, 2 * ELEMS, dtype=bf16)
HELD = ((5, 6, 7, 2, 3, 0, 1, 4), (1, 2, 0, 4, 5, 6, 7, 3))
PACKED = (
    (0, (5, 0), (1, 1)), (0, (6, 1), (2, 0)), (1, (4, 0), (2, 1)), (1, (5, 1), (3, 0)),
    (2, (7, 0), (0, 0)), (3, (6, 0), (0, 1)), (3, (7, 1), (1, 0)), (4, (4, 1), (3, 1)),
)
SCRATCH = [
    pltpu.VMEM((LEV, TALL, DEPTH), bf16),
    pltpu.VMEM((LEV, 8 * WIDE, LANES), f32),
    pltpu.VMEM((LEV, 8 * WIDE, LANES), f32),
]


def kept(value):
    return pltpu.with_memory_space_constraint(value, pltpu.VMEM)


def join(mine, theirs, both):
    both[0] = mine[...]
    both[1] = theirs[...]


def fetch(source, target, done):
    copy = pltpu.make_async_copy(source, target, done)
    copy.start()
    copy.wait()


def call(body, inputs, outs, scratch=(), smem=(), outside=(), keep=True):
    inputs = [pltpu.with_memory_space_constraint(x, pltpu.HBM) if i in outside else x for i, x in enumerate(inputs)]
    return pl.pallas_call(
        body,
        in_specs=[SMEM if i in smem else HBM if i in outside else VMEM for i in range(len(inputs))],
        out_specs=jax.tree.map(lambda _: VMEM, outs),
        out_shape=jax.tree.map(lambda o: pltpu.VMEM(o.shape, o.dtype), outs) if keep else outs,
        scratch_shapes=list(scratch),
        compiler_params=pltpu.CompilerParams(vmem_limit_bytes=12 << 20),
    )(*inputs)


def on_device(tracers, weights, departure, needs, counts):
    me = lax.axis_index("sfc")[None] % 2
    levels = jnp.transpose(tracers, (1, 0, 2))
    lists = jnp.transpose(needs[0], (1, 0))
    partner_lists = kept(swapped(lists))
    lists = kept(call(fetch, [lists], shaped(CAP, 2 * REACH, dtype=jnp.int32), [pltpu.SemaphoreType.DMA(())],
                      outside=(0,)))
    both = kept(call(join, [lists, partner_lists], shaped(2, CAP, 2 * REACH, dtype=jnp.int32)))
    asked2 = kept(ahead(both, 2))
    asked1 = kept(ahead(both, 1))
    other = kept(swapped(levels))
    table, hot, turned, levels = map(kept, call(
        prepare,
        [me, counts, levels, jnp.transpose(weights, (0, 2, 1, 3)), jnp.transpose(departure, (1, 0))],
        (TABLE, shaped(LEV, PAIRS, DEPTH, 2 * LANES, dtype=bf16), shaped(SUBSTEPS, LEV, LANES, LANES),
         shaped(LEV, ELEMS, ROW)),
        [pltpu.VMEM((TALL, LANES), f32), pltpu.SMEM((1, 2 * REACH), jnp.int32),
         pltpu.VMEM((SUBSTEPS, LEV, ELEMS, NODES * NODES), f32), pltpu.VMEM((LEV * NODES, ELEMS), jnp.int32),
         pltpu.SemaphoreType.DMA((4,))], smem=(0,), outside=(1, 2, 3, 4)))
    asked = [asked2, asked1, lists]
    for step in range(SUBSTEPS):
        width = TALL if step else ROW
        near, far, inner = call(
            lambda *refs: pack(width, *refs), [me] + asked + [levels, other],
            (shaped(2, LEV, 2 * CAP, TALL), shaped(3, LEV, CAP, TALL), shaped(LEV, CAP, TALL)), smem=(0,))
        far = kept(ahead(far, -2))
        near = kept(ahead(near, -1))
        inner = kept(inner)
        if step:
            table = kept(call(retable, [levels], TABLE))
        far_other = kept(swapped(far))
        near_other = kept(swapped(near))
        last = step + 1 == SUBSTEPS
        levels = call(
            lambda *refs: substep(step, *refs),
            [near, far, near_other, far_other, inner, table, hot, turned],
            shaped(LEV, ELEMS, ROW if last else TALL), SCRATCH, keep=not last)
        if not last:
            levels = kept(levels)
            other = kept(swapped(levels))
    return jnp.transpose(levels, (1, 0, 2))


def solution(mesh):
    return jax.shard_map(
        on_device,
        mesh=mesh,
        in_specs=(
            P("sfc", None, None),
            P(None, "sfc", None, None),
            P("sfc", None),
            P("sfc", None, None),
            P("sfc", None),
        ),
        out_specs=P("sfc", None, None),
        check_vma=False,
    )
```

profile of v0, /device:TPU:1, one launch (start us, length us, event | category | flops | bytes accessed | tf_op | source)
XLA Modules:
  0.0 45.3 jit_solution(16236336672236183491)
XLA Ops:
  0.0 1.4 %collective-permute-start.3 = (f32[3,64,480]{2,1,0:T(8,128)}, f32[3,64,480]{2,1,0:T(8,128)S(1)}, u32[]{:S(2)}, u32[]{:S(2)}) collective-permute-start(f32[3,64,480]{2,1,0:T(8,128)} %bitcast.9), channel_id=1, source_target_pairs={{0,1},{1,0},{2,3},{3,2},{4,5},{5,4},{6,7},{7,6},{8,9},{9,8},{10,11... | collective-permute-start | bytes 1105928 | tf_op jit(solution)/shard_map/ppermute | solution.py:34
  1.4 0.0 collective-permute-start
  1.4 0.7 %shard_map.55.mine.refs_3_ = s32[4,8]{1,0:T(4,128)S(1)} custom-call(s32[4,8]{1,0:T(4,128)} %bitcast.13), custom_call_target="tpu_custom_call" | custom-call | tf_op jit(solution)/shard_map/pallas_call | solution.py:202
  2.1 0.9 %collective-permute-done.theirs = s32[4,8]{1,0:T(4,128)S(1)} collective-permute-done((s32[4,8]{1,0:T(4,128)}, s32[4,8]{1,0:T(4,128)S(1)}, u32[]{:S(2)}, u32[]{:S(2)}) %collective-permute-start) | collective-permute-done | bytes 160 | tf_op jit(solution)/shard_map/ppermute | solution.py:34
  2.9 8.5 %collective-permute-start.2 = (s32[2,4,8]{2,1,0:T(4,128)S(1)}, s32[2,4,8]{2,1,0:T(4,128)S(1)}, u32[]{:S(2)}, u32[]{:S(2)}) collective-permute-start(s32[2,4,8]{2,1,0:T(4,128)S(1)} %shard_map.56), channel_id=1, source_target_pairs={{0,2},{1,127},{2,4},{3,1},{4,6},{5,3},{6,8},{7,5},{8,10},{9,7},{10... | collective-permute-start | bytes 776 | tf_op jit(solution)/shard_map/ppermute | solution.py:34
  11.5 0.5 %collective-permute-start.1 = (s32[2,4,8]{2,1,0:T(4,128)S(1)}, s32[2,4,8]{2,1,0:T(4,128)S(1)}, u32[]{:S(2)}, u32[]{:S(2)}) collective-permute-start(s32[2,4,8]{2,1,0:T(4,128)S(1)} %shard_map.56), channel_id=1, source_target_pairs={{0,4},{1,125},{2,6},{3,127},{4,8},{5,1},{6,10},{7,3},{8,12},{9,5},... | collective-permute-start | bytes 776 | tf_op jit(solution)/shard_map/ppermute | solution.py:34
  12.0 1.7 %shard_map.57 = (bf16[3,512,128]{2,1,0:T(8,128)(2,1)S(1)}, bf16[3,4,192,256]{3,2,1,0:T(8,128)(2,1)S(1)}, f32[2,3,128,128]{3,2,1,0:T(8,128)S(1)}, f32[3,64,480]{2,1,0:T(8,128)S(1)}) custom-call(s32[1]{0:T(128)S(6)} %select_n.7.me.refs_0_, s32[1,8]{1,0:T(1,128)} %counts_in.1, f32[3,64,480]{2,1,0:T(8,128)} %bitcast.10, f32[2,3,64,256]{3,2,1,0:T(8,128)} %bitcast.8, ...), custom_call_target="tpu_custom_call" | custom-call | tf_op jit(solution)/shard_map/pallas_call | solution.py:202
  13.7 0.0 collective-permute-done.2.refs_2_
  13.7 1.8 %collective-permute-done.1.refs_1_ = s32[2,4,8]{2,1,0:T(4,128)S(1)} collective-permute-done((s32[2,4,8]{2,1,0:T(4,128)S(1)}, s32[2,4,8]{2,1,0:T(4,128)S(1)}, u32[]{:S(2)}, u32[]{:S(2)}) %collective-permute-start.1) | collective-permute-done | bytes 288 | tf_op jit(solution)/shard_map/ppermute | solution.py:34
  15.5 0.0 collective-permute-done.3.refs_5_
  15.5 0.6 %shard_map.58 = (f32[2,3,8,512]{3,2,1,0:T(8,128)S(1)}, f32[3,3,4,512]{3,2,1,0:T(4,128)S(1)}, f32[3,4,512]{2,1,0:T(4,128)S(1)}) custom-call(s32[1]{0:T(128)S(6)} %select_n.7.me.refs_0_, s32[2,4,8]{2,1,0:T(4,128)S(1)} %collective-permute-done.1.refs_1_, s32[2,4,8]{2,1,0:T(4,128)S(1)} %collective-permute-done.2.refs_2_, s32[4,8]{1,0:T(4,128)S(1)} %shard_map.55.mine.refs_3_, ...), custom_call_target="tpu_custom_call" | custom-call | tf_op jit(solution)/shard_map/pallas_call | solution.py:202
  16.1 0.1 collective-permute-start.4
  16.2 0.7 %collective-permute-start.5 = (f32[3,3,4,512]{3,2,1,0:T(4,128)S(1)}, f32[3,3,4,512]{3,2,1,0:T(4,128)S(1)}, u32[]{:S(2)}, u32[]{:S(2)}) collective-permute-start(f32[3,3,4,512]{3,2,1,0:T(4,128)S(1)} %get-tuple-element.17), channel_id=1, source_target_pairs={{0,124},{1,5},{2,126},{3,7},{4,0},{5,9},{6,2},{7,11},{8,4},{9,13},... | collective-permute-start | bytes 221192 | tf_op jit(solution)/shard_map/ppermute | solution.py:34
  16.9 9.6 %collective-permute-done.4.refs_0_ = f32[2,3,8,512]{3,2,1,0:T(8,128)S(1)} collective-permute-done((f32[2,3,8,512]{3,2,1,0:T(8,128)S(1)}, f32[2,3,8,512]{3,2,1,0:T(8,128)S(1)}, u32[]{:S(2)}, u32[]{:S(2)}) %collective-permute-start.4) | collective-permute-done | bytes 98336 | tf_op jit(solution)/shard_map/ppermute | solution.py:34
  26.5 0.0 collective-permute-start.6
  26.5 0.0 collective-permute-done.5.refs_1_
  26.5 0.5 %collective-permute-start.7 = (f32[3,3,4,512]{3,2,1,0:T(4,128)S(1)}, f32[3,3,4,512]{3,2,1,0:T(4,128)S(1)}, u32[]{:S(2)}, u32[]{:S(2)}) collective-permute-start(f32[3,3,4,512]{3,2,1,0:T(4,128)S(1)} %collective-permute-done.5.refs_1_), channel_id=1, source_target_pairs={{0,1},{1,0},{2,3},{3,2},{4,5},{5,4},{6,7},{7,6},{8,9},{9,8},{10,11... | collective-permute-start | bytes 221192 | tf_op jit(solution)/shard_map/ppermute | solution.py:34
  27.0 0.9 %collective-permute-done.7.refs_3_ = f32[3,3,4,512]{3,2,1,0:T(4,128)S(1)} collective-permute-done((f32[3,3,4,512]{3,2,1,0:T(4,128)S(1)}, f32[3,3,4,512]{3,2,1,0:T(4,128)S(1)}, u32[]{:S(2)}, u32[]{:S(2)}) %collective-permute-start.7) | collective-permute-done | bytes 73760 | tf_op jit(solution)/shard_map/ppermute | solution.py:34
  27.9 0.0 collective-permute-done.6.refs_2_
  27.9 1.6 %shard_map.59.refs_4_.tracers = f32[3,64,512]{2,1,0:T(8,128)S(1)} custom-call(f32[2,3,8,512]{3,2,1,0:T(8,128)S(1)} %collective-permute-done.4.refs_0_, f32[3,3,4,512]{3,2,1,0:T(4,128)S(1)} %collective-permute-done.5.refs_1_, f32[2,3,8,512]{3,2,1,0:T(8,128)S(1)} %collective-permute-done.6.refs_2_, f32[3,3,4,512]{3,2,1,0:T(4,128)S(1)} %collective-permute-done.7.refs_3_, ...), custom_call_target="tpu_custom_call" | custom-call | tf_op jit(solution)/shard_map/pallas_call | solution.py:202
  29.5 0.4 collective-permute-start.8
  30.0 1.4 %collective-permute-done.8.refs_5_ = f32[3,64,512]{2,1,0:T(8,128)S(1)} collective-permute-done((f32[3,64,512]{2,1,0:T(8,128)S(1)}, f32[3,64,512]{2,1,0:T(8,128)S(1)}, u32[]{:S(2)}, u32[]{:S(2)}) %collective-permute-start.8) | collective-permute-done | bytes 393248 | tf_op jit(solution)/shard_map/ppermute | solution.py:34
  31.3 0.4 shard_map.60
  31.7 0.0 collective-permute-start.9
  31.8 0.1 collective-permute-start.10
  31.8 9.6 %collective-permute-done.9.refs_0_ = f32[2,3,8,512]{3,2,1,0:T(8,128)S(1)} collective-permute-done((f32[2,3,8,512]{3,2,1,0:T(8,128)S(1)}, f32[2,3,8,512]{3,2,1,0:T(8,128)S(1)}, u32[]{:S(2)}, u32[]{:S(2)}) %collective-permute-start.9) | collective-permute-done | bytes 98336 | tf_op jit(solution)/shard_map/ppermute | solution.py:34
  41.4 0.0 collective-permute-start.11
  41.4 0.0 collective-permute-done.10.refs_1_
  41.4 0.5 %collective-permute-start.12 = (f32[3,3,4,512]{3,2,1,0:T(4,128)S(1)}, f32[3,3,4,512]{3,2,1,0:T(4,128)S(1)}, u32[]{:S(2)}, u32[]{:S(2)}) collective-permute-start(f32[3,3,4,512]{3,2,1,0:T(4,128)S(1)} %collective-permute-done.10.refs_1_), channel_id=1, source_target_pairs={{0,1},{1,0},{2,3},{3,2},{4,5},{5,4},{6,7},{7,6},{8,9},{9,8},{10,11... | collective-permute-start | bytes 221192 | tf_op jit(solution)/shard_map/ppermute | solution.py:34
  42.0 0.2 shard_map.61.refs_5_
  42.1 0.7 %collective-permute-done.12.refs_3_ = f32[3,3,4,512]{3,2,1,0:T(4,128)S(1)} collective-permute-done((f32[3,3,4,512]{3,2,1,0:T(4,128)S(1)}, f32[3,3,4,512]{3,2,1,0:T(4,128)S(1)}, u32[]{:S(2)}, u32[]{:S(2)}) %collective-permute-start.12) | collective-permute-done | bytes 73760 | tf_op jit(solution)/shard_map/ppermute | solution.py:34
  42.9 0.0 collective-permute-done.11.refs_2_
  42.9 2.4 %shard_map.62 = f32[3,64,480]{2,1,0:T(8,128)} custom-call(f32[2,3,8,512]{3,2,1,0:T(8,128)S(1)} %collective-permute-done.9.refs_0_, f32[3,3,4,512]{3,2,1,0:T(4,128)S(1)} %collective-permute-done.10.refs_1_, f32[2,3,8,512]{3,2,1,0:T(8,128)S(1)} %collective-permute-done.11.refs_2_, f32[3,3,4,512]{3,2,1,0:T(4,128)S(1)} %collective-permute-done.12.refs_3_, ...), custom_call_target="tpu_custom_call" | custom-call | tf_op jit(solution)/shard_map/pallas_call | solution.py:202
  (1 shorter events, 0.0 us)
Async XLA Ops:
  0.0 15.5 %collective-permute-start.3 = (f32[3,64,480]{2,1,0:T(8,128)}, f32[3,64,480]{2,1,0:T(8,128)S(1)}, u32[]{:S(2)}, u32[]{:S(2)}) collective-permute-start(f32[3,64,480]{2,1,0:T(8,128)} %bitcast.9), channel_id=1, source_target_pairs={{0,1},{1,0},{2,3},{3,2},{4,5},{5,4},{6,7},{7,6},{8,9},{9,8},{10,11... | collective-permute-start | bytes 1105928 | tf_op jit(solution)/shard_map/ppermute | solution.py:34
  1.4 1.6 %collective-permute-start = (s32[4,8]{1,0:T(4,128)}, s32[4,8]{1,0:T(4,128)S(1)}, u32[]{:S(2)}, u32[]{:S(2)}) collective-permute-start(s32[4,8]{1,0:T(4,128)} %bitcast.12), channel_id=1, source_target_pairs={{0,1},{1,0},{2,3},{3,2},{4,5},{5,4},{6,7},{7,6},{8,9},{9,8},{10,11... | collective-permute-start | bytes 392 | tf_op jit(solution)/shard_map/ppermute | solution.py:34
  2.9 10.7 %collective-permute-start.2 = (s32[2,4,8]{2,1,0:T(4,128)S(1)}, s32[2,4,8]{2,1,0:T(4,128)S(1)}, u32[]{:S(2)}, u32[]{:S(2)}) collective-permute-start(s32[2,4,8]{2,1,0:T(4,128)S(1)} %shard_map.56), channel_id=1, source_target_pairs={{0,2},{1,127},{2,4},{3,1},{4,6},{5,3},{6,8},{7,5},{8,10},{9,7},{10... | collective-permute-start | bytes 776 | tf_op jit(solution)/shard_map/ppermute | solution.py:34
  11.5 4.1 %collective-permute-start.1 = (s32[2,4,8]{2,1,0:T(4,128)S(1)}, s32[2,4,8]{2,1,0:T(4,128)S(1)}, u32[]{:S(2)}, u32[]{:S(2)}) collective-permute-start(s32[2,4,8]{2,1,0:T(4,128)S(1)} %shard_map.56), channel_id=1, source_target_pairs={{0,4},{1,125},{2,6},{3,127},{4,8},{5,1},{6,10},{7,3},{8,12},{9,5},... | collective-permute-start | bytes 776 | tf_op jit(solution)/shard_map/ppermute | solution.py:34
  16.1 10.4 %collective-permute-start.4 = (f32[2,3,8,512]{3,2,1,0:T(8,128)S(1)}, f32[2,3,8,512]{3,2,1,0:T(8,128)S(1)}, u32[]{:S(2)}, u32[]{:S(2)}) collective-permute-start(f32[2,3,8,512]{3,2,1,0:T(8,128)S(1)} %get-tuple-element.16), channel_id=1, source_target_pairs={{0,126},{1,3},{2,0},{3,5},{4,2},{5,7},{6,4},{7,9},{8,6},{9,11},{10... | collective-permute-start | bytes 294920 | tf_op jit(solution)/shard_map/ppermute | solution.py:34
  16.2 10.3 %collective-permute-start.5 = (f32[3,3,4,512]{3,2,1,0:T(4,128)S(1)}, f32[3,3,4,512]{3,2,1,0:T(4,128)S(1)}, u32[]{:S(2)}, u32[]{:S(2)}) collective-permute-start(f32[3,3,4,512]{3,2,1,0:T(4,128)S(1)} %get-tuple-element.17), channel_id=1, source_target_pairs={{0,124},{1,5},{2,126},{3,7},{4,0},{5,9},{6,2},{7,11},{8,4},{9,13},... | collective-permute-start | bytes 221192 | tf_op jit(solution)/shard_map/ppermute | solution.py:34
  26.5 1.4 %collective-permute-start.6 = (f32[2,3,8,512]{3,2,1,0:T(8,128)S(1)}, f32[2,3,8,512]{3,2,1,0:T(8,128)S(1)}, u32[]{:S(2)}, u32[]{:S(2)}) collective-permute-start(f32[2,3,8,512]{3,2,1,0:T(8,128)S(1)} %collective-permute-done.4.refs_0_), channel_id=1, source_target_pairs={{0,1},{1,0},{2,3},{3,2},{4,5},{5,4},{6,7},{7,6},{8,9},{9,8},{10,11... | collective-permute-start | bytes 294920 | tf_op jit(solution)/shard_map/ppermute | solution.py:34
  26.5 1.4 %collective-permute-start.7 = (f32[3,3,4,512]{3,2,1,0:T(4,128)S(1)}, f32[3,3,4,512]{3,2,1,0:T(4,128)S(1)}, u32[]{:S(2)}, u32[]{:S(2)}) collective-permute-start(f32[3,3,4,512]{3,2,1,0:T(4,128)S(1)} %collective-permute-done.5.refs_1_), channel_id=1, source_target_pairs={{0,1},{1,0},{2,3},{3,2},{4,5},{5,4},{6,7},{7,6},{8,9},{9,8},{10,11... | collective-permute-start | bytes 221192 | tf_op jit(solution)/shard_map/ppermute | solution.py:34
  29.5 1.8 %collective-permute-start.8 = (f32[3,64,512]{2,1,0:T(8,128)S(1)}, f32[3,64,512]{2,1,0:T(8,128)S(1)}, u32[]{:S(2)}, u32[]{:S(2)}) collective-permute-start(f32[3,64,512]{2,1,0:T(8,128)S(1)} %shard_map.59.refs_4_.tracers), channel_id=1, source_target_pairs={{0,1},{1,0},{2,3},{3,2},{4,5},{5,4},{6,7},{7,6},{8,9},{9,8},{10,11... | collective-permute-start | bytes 1179656 | tf_op jit(solution)/shard_map/ppermute | solution.py:34
  31.7 9.7 %collective-permute-start.9 = (f32[2,3,8,512]{3,2,1,0:T(8,128)S(1)}, f32[2,3,8,512]{3,2,1,0:T(8,128)S(1)}, u32[]{:S(2)}, u32[]{:S(2)}) collective-permute-start(f32[2,3,8,512]{3,2,1,0:T(8,128)S(1)} %get-tuple-element.22), channel_id=1, source_target_pairs={{0,126},{1,3},{2,0},{3,5},{4,2},{5,7},{6,4},{7,9},{8,6},{9,11},{10... | collective-permute-start | bytes 294920 | tf_op jit(solution)/shard_map/ppermute | solution.py:34
  31.8 9.7 %collective-permute-start.10 = (f32[3,3,4,512]{3,2,1,0:T(4,128)S(1)}, f32[3,3,4,512]{3,2,1,0:T(4,128)S(1)}, u32[]{:S(2)}, u32[]{:S(2)}) collective-permute-start(f32[3,3,4,512]{3,2,1,0:T(4,128)S(1)} %get-tuple-element.23), channel_id=1, source_target_pairs={{0,124},{1,5},{2,126},{3,7},{4,0},{5,9},{6,2},{7,11},{8,4},{9,13},... | collective-permute-start | bytes 221192 | tf_op jit(solution)/shard_map/ppermute | solution.py:34
  41.4 1.4 %collective-permute-start.11 = (f32[2,3,8,512]{3,2,1,0:T(8,128)S(1)}, f32[2,3,8,512]{3,2,1,0:T(8,128)S(1)}, u32[]{:S(2)}, u32[]{:S(2)}) collective-permute-start(f32[2,3,8,512]{3,2,1,0:T(8,128)S(1)} %collective-permute-done.9.refs_0_), channel_id=1, source_target_pairs={{0,1},{1,0},{2,3},{3,2},{4,5},{5,4},{6,7},{7,6},{8,9},{9,8},{10,11... | collective-permute-start | bytes 294920 | tf_op jit(solution)/shard_map/ppermute | solution.py:34
  41.4 1.4 %collective-permute-start.12 = (f32[3,3,4,512]{3,2,1,0:T(4,128)S(1)}, f32[3,3,4,512]{3,2,1,0:T(4,128)S(1)}, u32[]{:S(2)}, u32[]{:S(2)}) collective-permute-start(f32[3,3,4,512]{3,2,1,0:T(4,128)S(1)} %collective-permute-done.10.refs_1_), channel_id=1, source_target_pairs={{0,1},{1,0},{2,3},{3,2},{4,5},{5,4},{6,7},{7,6},{8,9},{9,8},{10,11... | collective-permute-start | bytes 221192 | tf_op jit(solution)/shard_map/ppermute | solution.py:34
where the time goes:
time: 45.4 us; the launch traced here: 45.3 us
  waiting for transfers between devices  24.9 us (55%)
  starting transfers between devices  12.8 us (28%)
  Pallas kernels  7.59 us (17%)
    ppermute x13, waiting for transfers between devices, moved(): lax.ppermute(value, 'sfc', [(source, target(source) % N) for source in ra...  24.9 us
    ppermute x13, starting transfers between devices, moved(): lax.ppermute(value, 'sfc', [(source, target(source) % N) for source in ra...  12.8 us
    pallas_call x8, Pallas kernels, call(): pl.pallas_call(body, in_specs=[SMEM if i in smem else HBM if i in outside...  7.59 us
  transfers between devices with their start and end apart: 13, of which 7 were waited for; matrix products, arithmetic and copies ran while one was open for 0% of the time, Pallas kernels for 6%

commit v1 on v0

--- a/solution.py
+++ b/solution.py
@@ -47,16 +47,15 @@
     return high, x - high
 
 
-def prepare(me, counts_in, tracers_in, weights_in, departure_in, table, hot, turned, tracers,
+def prepare(me, tracers, counts_in, weights_in, departure_in, table, hot, turned,
             spaced, counts, weights, departure, done):
     copies = [pltpu.make_async_copy(source, target, done.at[i]) for i, (source, target) in enumerate(
-        [(tracers_in, tracers), (counts_in, counts), (departure_in, departure), (weights_in, weights)])]
+        [(counts_in, counts), (departure_in, departure), (weights_in, weights)])]
     for copy in copies:
         copy.start()
     spaced[ROW:, :] = jnp.zeros_like(spaced[ROW:, :])
     copies[0].wait()
     copies[1].wait()
-    copies[2].wait()
     slot = lax.broadcasted_iota(jnp.int32, (REMOTE, LANES), 0)
     group, entry = slot // CAP, slot % CAP
     limit = base = jnp.zeros_like(slot)
@@ -80,14 +79,14 @@
             far = (far_slot == row).astype(f32).astype(bf16)
             lanes = slice((t % 2) * LANES, (t % 2 + 1) * LANES)
             hot[level, t // 2, :, lanes] = jnp.concatenate([near, near, far, far], axis=0)
-    copies[3].wait()
+    copies[2].wait()
     for level in range(LEV):
         for step in range(SUBSTEPS):
             both = jnp.concatenate([weights[step, level, :, 0:LANES], weights[step, level, :, LANES:2 * LANES]], axis=0)
             turned[step, level] = both.T
 
 
-def pack(width, me, asked2, asked1, lists, own, other, near, far, inner):
+def pack(me, asked2, asked1, lists, own, other, near, far, inner):
     lane = lax.broadcasted_iota(jnp.int32, (CAP, LANES), 1)
     sources = [asked1.at[0], asked1.at[1], asked2.at[0], asked2.at[1], lists]
     picks = []
@@ -96,45 +95,57 @@
         picks.append((jnp.broadcast_to(jnp.where(me[0] == 0, one[0], one[1]), (CAP, LANES)) == lane).astype(f32))
     picks = jnp.concatenate(picks, axis=0).astype(bf16)
     picks = jnp.concatenate([picks, picks, picks], axis=1)
-
-    def give(level, lanes, rows):
-        near[0, level, :, lanes] = rows[0:8]
-        near[1, level, :, lanes] = rows[8:16]
-        for g in range(3):
-            far[g, level, :, lanes] = rows[16 + 4 * g:20 + 4 * g]
-        inner[level, :, lanes] = rows[28:32]
-
-    for level in range(LEV):
-        both = jnp.concatenate([own[level], other[level]], axis=0)
-        high, rest = split(both)
+    for level in range(LEV):
+        high, rest = split(jnp.concatenate([own[level], other[level]], axis=0))
         middle, low = split(rest)
         parts = jnp.concatenate([high.astype(bf16), middle.astype(bf16), low.astype(bf16)], axis=0)
         rows = jnp.dot(picks, parts, preferred_element_type=f32)
-        if width == TALL:
-            give(level, slice(0, TALL), rows)
-        else:
-            spread = []
-            for k in range(NODES):
-                spread += [rows[:, k * TRACERS:(k + 1) * TRACERS], jnp.zeros((REMOTE, WIDE - TRACERS), f32)]
-            give(level, slice(0, TALL), jnp.concatenate(spread, axis=1))
-
-
-def substep(step, near, far, near_other, far_other, inner, table, hot, turned, out, whole, mixed, close):
+        near[0, level] = rows[0:8]
+        near[1, level] = rows[8:16]
+        for g in range(3):
+            far[g, level] = rows[16 + 4 * g:20 + 4 * g]
+        inner[level] = rows[28:32]
+
+
+def substep(step, near, far, near_other, far_other, inner, table, hot, turned, out, whole, mixed, close, spaced, rowed, done):
     last = step + 1 == SUBSTEPS
-    for level in range(LEV):
+    half = 8 * TRACERS
+    spaced[:, ROW:, :] = jnp.zeros_like(spaced[:, ROW:, :])
+
+    def assemble(level):
         rows = jnp.concatenate(
             [near[0, level], far[0, level], near_other[1, level], far_other[1, level], far_other[2, level], inner[level]],
             axis=0)
         high, low = split(rows)
         whole[level, :, 0:2 * ELEMS] = table[level]
-        whole[level, :, 2 * ELEMS:] = jnp.concatenate([high, low], axis=0).T.astype(bf16)
-
+        columns = jnp.concatenate([high, low], axis=0).T
+        if step:
+            whole[level, :, 2 * ELEMS:] = columns.astype(bf16)
+        else:
+            spaced[level, 0:ROW, :] = columns
+            for k in range(NODES):
+                whole[level, k * WIDE:(k + 1) * WIDE, 2 * ELEMS:] = spaced[
+                    level, k * TRACERS:k * TRACERS + WIDE, :].astype(bf16)
+
+    def give(level):
+        if last:
+            rows = close[level].T
+            rowed[level, :, 0:half] = rows[:ELEMS, 0:half]
+            rowed[level, :, half:2 * half] = rows[ELEMS:, 0:half]
+            pltpu.make_async_copy(rowed.at[level], out.at[level], done.at[level]).start()
+        else:
+            rows = mixed[level].T
+            out[level, :, 0:8 * WIDE] = rows[:ELEMS]
+            out[level, :, 8 * WIDE:] = rows[ELEMS:]
+
+    for level in range(LEV):
+        assemble(level)
     for level in range(LEV):
         for pair in range(PAIRS):
             gathered = jnp.dot(whole[level], hot[level, pair], preferred_element_type=f32)
-            for half in range(2):
-                lanes = slice(half * LANES, (half + 1) * LANES)
-                t = pair * 2 + half
+            for side in range(2):
+                lanes = slice(side * LANES, (side + 1) * LANES)
+                t = pair * 2 + side
                 factors = turned[step, level, t * NODES:(t + 1) * NODES, :]
                 total = lowest = highest = None
                 for k in range(NODES):
@@ -148,15 +159,10 @@
                     close[level, t * TRACERS:(t + 1) * TRACERS, :] = result[:TRACERS]
                 else:
                     mixed[level, t * WIDE:(t + 1) * WIDE, :] = result
-        if last:
-            rows = close[level].T
-            half = 8 * TRACERS
-            out[level, :, 0:half] = rows[:ELEMS, 0:half]
-            out[level, :, half:2 * half] = rows[ELEMS:, 0:half]
-        else:
-            rows = mixed[level].T
-            out[level, :, 0:8 * WIDE] = rows[:ELEMS]
-            out[level, :, 8 * WIDE:] = rows[ELEMS:]
+        give(level)
+    if last:
+        for level in range(LEV):
+            pltpu.make_async_copy(rowed.at[level], out.at[level], done.at[level]).wait()
 
 
 def retable(tracers, table):
@@ -179,6 +185,9 @@
     pltpu.VMEM((LEV, TALL, DEPTH), bf16),
     pltpu.VMEM((LEV, 8 * WIDE, LANES), f32),
     pltpu.VMEM((LEV, 8 * WIDE, LANES), f32),
+    pltpu.VMEM((LEV, TALL, 2 * REMOTE), f32),
+    pltpu.VMEM((LEV, ELEMS, ROW), f32),
+    pltpu.SemaphoreType.DMA((LEV,)),
 ]
 
 
@@ -202,7 +211,7 @@
     return pl.pallas_call(
         body,
         in_specs=[SMEM if i in smem else HBM if i in outside else VMEM for i in range(len(inputs))],
-        out_specs=jax.tree.map(lambda _: VMEM, outs),
+        out_specs=jax.tree.map(lambda _: VMEM if keep else HBM, outs),
         out_shape=jax.tree.map(lambda o: pltpu.VMEM(o.shape, o.dtype), outs) if keep else outs,
         scratch_shapes=list(scratch),
         compiler_params=pltpu.CompilerParams(vmem_limit_bytes=12 << 20),
@@ -214,34 +223,36 @@
     levels = jnp.transpose(tracers, (1, 0, 2))
     lists = jnp.transpose(needs[0], (1, 0))
     partner_lists = kept(swapped(lists))
+    other = kept(swapped(levels))
     lists = kept(call(fetch, [lists], shaped(CAP, 2 * REACH, dtype=jnp.int32), [pltpu.SemaphoreType.DMA(())],
                       outside=(0,)))
     both = kept(call(join, [lists, partner_lists], shaped(2, CAP, 2 * REACH, dtype=jnp.int32)))
     asked2 = kept(ahead(both, 2))
     asked1 = kept(ahead(both, 1))
-    other = kept(swapped(levels))
-    table, hot, turned, levels = map(kept, call(
-        prepare,
-        [me, counts, levels, jnp.transpose(weights, (0, 2, 1, 3)), jnp.transpose(departure, (1, 0))],
-        (TABLE, shaped(LEV, PAIRS, DEPTH, 2 * LANES, dtype=bf16), shaped(SUBSTEPS, LEV, LANES, LANES),
-         shaped(LEV, ELEMS, ROW)),
-        [pltpu.VMEM((TALL, LANES), f32), pltpu.SMEM((1, 2 * REACH), jnp.int32),
-         pltpu.VMEM((SUBSTEPS, LEV, ELEMS, NODES * NODES), f32), pltpu.VMEM((LEV * NODES, ELEMS), jnp.int32),
-         pltpu.SemaphoreType.DMA((4,))], smem=(0,), outside=(1, 2, 3, 4)))
     asked = [asked2, asked1, lists]
+    levels = kept(call(fetch, [levels], shaped(LEV, ELEMS, ROW), [pltpu.SemaphoreType.DMA(())], outside=(0,)))
     for step in range(SUBSTEPS):
+        last = step + 1 == SUBSTEPS
         width = TALL if step else ROW
         near, far, inner = call(
-            lambda *refs: pack(width, *refs), [me] + asked + [levels, other],
-            (shaped(2, LEV, 2 * CAP, TALL), shaped(3, LEV, CAP, TALL), shaped(LEV, CAP, TALL)), smem=(0,))
+            lambda *refs: pack(*refs), [me] + asked + [levels, other],
+            (shaped(2, LEV, 2 * CAP, width), shaped(3, LEV, CAP, width), shaped(LEV, CAP, width)),
+            smem=(0,))
         far = kept(ahead(far, -2))
         near = kept(ahead(near, -1))
         inner = kept(inner)
         if step:
             table = kept(call(retable, [levels], TABLE))
+        else:
+            table, hot, turned = map(kept, call(
+                prepare,
+                [me, levels, counts, jnp.transpose(weights, (0, 2, 1, 3)), jnp.transpose(departure, (1, 0))],
+                (TABLE, shaped(LEV, PAIRS, DEPTH, 2 * LANES, dtype=bf16), shaped(SUBSTEPS, LEV, LANES, LANES)),
+                [pltpu.VMEM((TALL, LANES), f32), pltpu.SMEM((1, 2 * REACH), jnp.int32),
+                 pltpu.VMEM((SUBSTEPS, LEV, ELEMS, NODES * NODES), f32), pltpu.VMEM((LEV * NODES, ELEMS), jnp.int32),
+                 pltpu.SemaphoreType.DMA((3,))], smem=(0,), outside=(2, 3, 4)))
         far_other = kept(swapped(far))
         near_other = kept(swapped(near))
-        last = step + 1 == SUBSTEPS
         levels = call(
             lambda *refs: substep(step, *refs),
             [near, far, near_other, far_other, inner, table, hot, turned],

time: 45.4 us -> 45.1 us (level)
  waiting for transfers between devices: 24.9 us -> 24.2 us
  Pallas kernels: 7.59 us -> 8.19 us
    ppermute x13, waiting for transfers between devices: 24.9 us -> 24.2 us  [moved(): lax.ppermute(value, 'sfc', [(source, target(source) % N) for source in ra...]
    pallas_call x8 -> x9, Pallas kernels: 7.59 us -> 8.19 us  [call(): pl.pallas_call(body, in_specs=[SMEM if i in smem else HBM if i in outside...]
  transfers between devices with their start and end apart: 13 -> 13, of which waited for: 7 -> 6; matrix products, arithmetic and copies ran while one was open for 0% -> 0% of each run, Pallas kernels for 6% -> 7%
where the time goes in v1:
time: 45.1 us; the launch traced here: 45 us
  waiting for transfers between devices  24.2 us (54%)
  starting transfers between devices  12.5 us (28%)
  Pallas kernels  8.19 us (18%)
    ppermute x13, waiting for transfers between devices, moved(): lax.ppermute(value, 'sfc', [(source, target(source) % N) for source in ra...  24.2 us
    ppermute x13, starting transfers between devices, moved(): lax.ppermute(value, 'sfc', [(source, target(source) % N) for source in ra...  12.5 us
    pallas_call x9, Pallas kernels, call(): pl.pallas_call(body, in_specs=[SMEM if i in smem else HBM if i in outside...  8.19 us
  transfers between devices with their start and end apart: 13, of which 6 were waited for; matrix products, arithmetic and copies ran while one was open for 0% of the time, Pallas kernels for 7%

profile of v1, /device:TPU:1, one launch (start us, length us, event | category | flops | bytes accessed | tf_op | source)
XLA Modules:
  0.0 45.0 jit_solution(3345940468591519298)
XLA Ops:
  0.0 1.4 %collective-permute-start.3 = (f32[3,64,480]{2,1,0:T(8,128)}, f32[3,64,480]{2,1,0:T(8,128)S(1)}, u32[]{:S(2)}, u32[]{:S(2)}) collective-permute-start(f32[3,64,480]{2,1,0:T(8,128)} %bitcast.8), channel_id=1, source_target_pairs={{0,1},{1,0},{2,3},{3,2},{4,5},{5,4},{6,7},{7,6},{8,9},{9,8},{10,11... | collective-permute-start | bytes 1105928 | tf_op jit(solution)/shard_map/ppermute | solution.py:34
  1.4 0.0 collective-permute-start
  1.4 0.7 %shard_map.55.mine.refs_3_ = s32[4,8]{1,0:T(4,128)S(1)} custom-call(s32[4,8]{1,0:T(4,128)} %bitcast.13), custom_call_target="tpu_custom_call" | custom-call | tf_op jit(solution)/shard_map/pallas_call | solution.py:211
  2.1 1.0 %shard_map.57.refs_4_.tracers = f32[3,64,480]{2,1,0:T(8,128)S(1)} custom-call(f32[3,64,480]{2,1,0:T(8,128)} %bitcast.9), custom_call_target="tpu_custom_call" | custom-call | tf_op jit(solution)/shard_map/pallas_call | solution.py:211
  3.1 0.0 collective-permute-done.theirs
  3.1 8.8 %collective-permute-start.1 = (s32[2,4,8]{2,1,0:T(4,128)S(1)}, s32[2,4,8]{2,1,0:T(4,128)S(1)}, u32[]{:S(2)}, u32[]{:S(2)}) collective-permute-start(s32[2,4,8]{2,1,0:T(4,128)S(1)} %shard_map.56), channel_id=1, source_target_pairs={{0,4},{1,125},{2,6},{3,127},{4,8},{5,1},{6,10},{7,3},{8,12},{9,5},... | collective-permute-start | bytes 776 | tf_op jit(solution)/shard_map/ppermute | solution.py:34
  12.0 0.9 %collective-permute-start.2 = (s32[2,4,8]{2,1,0:T(4,128)S(1)}, s32[2,4,8]{2,1,0:T(4,128)S(1)}, u32[]{:S(2)}, u32[]{:S(2)}) collective-permute-start(s32[2,4,8]{2,1,0:T(4,128)S(1)} %shard_map.56), channel_id=1, source_target_pairs={{0,2},{1,127},{2,4},{3,1},{4,6},{5,3},{6,8},{7,5},{8,10},{9,7},{10... | collective-permute-start | bytes 776 | tf_op jit(solution)/shard_map/ppermute | solution.py:34
  12.8 0.0 collective-permute-done.1.refs_1_
  12.8 1.9 %collective-permute-done.2.refs_2_ = s32[2,4,8]{2,1,0:T(4,128)S(1)} collective-permute-done((s32[2,4,8]{2,1,0:T(4,128)S(1)}, s32[2,4,8]{2,1,0:T(4,128)S(1)}, u32[]{:S(2)}, u32[]{:S(2)}) %collective-permute-start.2) | collective-permute-done | bytes 288 | tf_op jit(solution)/shard_map/ppermute | solution.py:34
  14.7 0.0 collective-permute-done.3.refs_5_
  14.7 0.4 shard_map.58
  15.1 0.0 collective-permute-start.4
  15.2 0.2 collective-permute-start.5
  15.3 9.4 %collective-permute-done.4.refs_0_ = f32[2,3,8,480]{3,2,1,0:T(8,128)S(1)} collective-permute-done((f32[2,3,8,480]{3,2,1,0:T(8,128)S(1)}, f32[2,3,8,480]{3,2,1,0:T(8,128)S(1)}, u32[]{:S(2)}, u32[]{:S(2)}) %collective-permute-start.4) | collective-permute-done | bytes 92192 | tf_op jit(solution)/shard_map/ppermute | solution.py:34
  24.7 0.0 collective-permute-start.6
  24.7 1.2 %collective-permute-done.5.refs_1_ = f32[3,3,4,480]{3,2,1,0:T(4,128)S(1)} collective-permute-done((f32[3,3,4,480]{3,2,1,0:T(4,128)S(1)}, f32[3,3,4,480]{3,2,1,0:T(4,128)S(1)}, u32[]{:S(2)}, u32[]{:S(2)}) %collective-permute-start.5) | collective-permute-done | bytes 69152 | tf_op jit(solution)/shard_map/ppermute | solution.py:34
  25.9 0.0 collective-permute-start.7
  25.9 1.4 %shard_map.59 = (bf16[3,512,128]{2,1,0:T(8,128)(2,1)S(1)}, bf16[3,4,192,256]{3,2,1,0:T(8,128)(2,1)S(1)}, f32[2,3,128,128]{3,2,1,0:T(8,128)S(1)}) custom-call(s32[1]{0:T(128)S(6)} %select_n.7.refs_0_.me, f32[3,64,480]{2,1,0:T(8,128)S(1)} %shard_map.57.refs_4_.tracers, s32[1,8]{1,0:T(1,128)} %counts_in.1, f32[2,3,64,256]{3,2,1,0:T(8,128)} %bitcast.10, ...), custom_call_target="tpu_custom_call" | custom-call | tf_op jit(solution)/shard_map/pallas_call | solution.py:211
  27.4 0.0 collective-permute-done.7.refs_3_
  27.4 0.0 collective-permute-done.6.refs_2_
  27.4 1.7 %shard_map.60.refs_4_.tracers = f32[3,64,512]{2,1,0:T(8,128)S(1)} custom-call(f32[2,3,8,480]{3,2,1,0:T(8,128)S(1)} %collective-permute-done.4.refs_0_, f32[3,3,4,480]{3,2,1,0:T(4,128)S(1)} %collective-permute-done.5.refs_1_, f32[2,3,8,480]{3,2,1,0:T(8,128)S(1)} %collective-permute-done.6.refs_2_, f32[3,3,4,480]{3,2,1,0:T(4,128)S(1)} %collective-permute-done.7.refs_3_, ...), custom_call_target="tpu_custom_call" | custom-call | tf_op jit(solution)/shard_map/pallas_call | solution.py:211
  29.1 0.6 %collective-permute-start.8 = (f32[3,64,512]{2,1,0:T(8,128)S(1)}, f32[3,64,512]{2,1,0:T(8,128)S(1)}, u32[]{:S(2)}, u32[]{:S(2)}) collective-permute-start(f32[3,64,512]{2,1,0:T(8,128)S(1)} %shard_map.60.refs_4_.tracers), channel_id=1, source_target_pairs={{0,1},{1,0},{2,3},{3,2},{4,5},{5,4},{6,7},{7,6},{8,9},{9,8},{10,11... | collective-permute-start | bytes 1179656 | tf_op jit(solution)/shard_map/ppermute | solution.py:34
  29.7 1.3 %collective-permute-done.8.refs_5_ = f32[3,64,512]{2,1,0:T(8,128)S(1)} collective-permute-done((f32[3,64,512]{2,1,0:T(8,128)S(1)}, f32[3,64,512]{2,1,0:T(8,128)S(1)}, u32[]{:S(2)}, u32[]{:S(2)}) %collective-permute-start.8) | collective-permute-done | bytes 393248 | tf_op jit(solution)/shard_map/ppermute | solution.py:34
  31.0 0.4 shard_map.61
  31.4 0.0 collective-permute-start.9
  31.5 0.1 collective-permute-start.10
  31.6 9.6 %collective-permute-done.9.refs_0_ = f32[2,3,8,512]{3,2,1,0:T(8,128)S(1)} collective-permute-done((f32[2,3,8,512]{3,2,1,0:T(8,128)S(1)}, f32[2,3,8,512]{3,2,1,0:T(8,128)S(1)}, u32[]{:S(2)}, u32[]{:S(2)}) %collective-permute-start.9) | collective-permute-done | bytes 98336 | tf_op jit(solution)/shard_map/ppermute | solution.py:34
  41.2 0.0 collective-permute-start.11
  41.2 0.0 collective-permute-done.10.refs_1_
  41.2 0.5 %collective-permute-start.12 = (f32[3,3,4,512]{3,2,1,0:T(4,128)S(1)}, f32[3,3,4,512]{3,2,1,0:T(4,128)S(1)}, u32[]{:S(2)}, u32[]{:S(2)}) collective-permute-start(f32[3,3,4,512]{3,2,1,0:T(4,128)S(1)} %collective-permute-done.10.refs_1_), channel_id=1, source_target_pairs={{0,1},{1,0},{2,3},{3,2},{4,5},{5,4},{6,7},{7,6},{8,9},{9,8},{10,11... | collective-permute-start | bytes 221192 | tf_op jit(solution)/shard_map/ppermute | solution.py:34
  41.7 0.2 shard_map.62.refs_5_
  41.8 0.7 %collective-permute-done.12.refs_3_ = f32[3,3,4,512]{3,2,1,0:T(4,128)S(1)} collective-permute-done((f32[3,3,4,512]{3,2,1,0:T(4,128)S(1)}, f32[3,3,4,512]{3,2,1,0:T(4,128)S(1)}, u32[]{:S(2)}, u32[]{:S(2)}) %collective-permute-start.12) | collective-permute-done | bytes 73760 | tf_op jit(solution)/shard_map/ppermute | solution.py:34
  42.6 0.0 collective-permute-done.11.refs_2_
  42.6 2.4 %shard_map.63 = f32[3,64,480]{2,1,0:T(8,128)} custom-call(f32[2,3,8,512]{3,2,1,0:T(8,128)S(1)} %collective-permute-done.9.refs_0_, f32[3,3,4,512]{3,2,1,0:T(4,128)S(1)} %collective-permute-done.10.refs_1_, f32[2,3,8,512]{3,2,1,0:T(8,128)S(1)} %collective-permute-done.11.refs_2_, f32[3,3,4,512]{3,2,1,0:T(4,128)S(1)} %collective-permute-done.12.refs_3_, ...), custom_call_target="tpu_custom_call" | custom-call | tf_op jit(solution)/shard_map/pallas_call | solution.py:211
  (1 shorter events, 0.0 us)
Async XLA Ops:
  0.0 14.7 %collective-permute-start.3 = (f32[3,64,480]{2,1,0:T(8,128)}, f32[3,64,480]{2,1,0:T(8,128)S(1)}, u32[]{:S(2)}, u32[]{:S(2)}) collective-permute-start(f32[3,64,480]{2,1,0:T(8,128)} %bitcast.8), channel_id=1, source_target_pairs={{0,1},{1,0},{2,3},{3,2},{4,5},{5,4},{6,7},{7,6},{8,9},{9,8},{10,11... | collective-permute-start | bytes 1105928 | tf_op jit(solution)/shard_map/ppermute | solution.py:34
  1.4 1.7 %collective-permute-start = (s32[4,8]{1,0:T(4,128)}, s32[4,8]{1,0:T(4,128)S(1)}, u32[]{:S(2)}, u32[]{:S(2)}) collective-permute-start(s32[4,8]{1,0:T(4,128)} %bitcast.12), channel_id=1, source_target_pairs={{0,1},{1,0},{2,3},{3,2},{4,5},{5,4},{6,7},{7,6},{8,9},{9,8},{10,11... | collective-permute-start | bytes 392 | tf_op jit(solution)/shard_map/ppermute | solution.py:34
  3.1 9.7 %collective-permute-start.1 = (s32[2,4,8]{2,1,0:T(4,128)S(1)}, s32[2,4,8]{2,1,0:T(4,128)S(1)}, u32[]{:S(2)}, u32[]{:S(2)}) collective-permute-start(s32[2,4,8]{2,1,0:T(4,128)S(1)} %shard_map.56), channel_id=1, source_target_pairs={{0,4},{1,125},{2,6},{3,127},{4,8},{5,1},{6,10},{7,3},{8,12},{9,5},... | collective-permute-start | bytes 776 | tf_op jit(solution)/shard_map/ppermute | solution.py:34
  12.0 2.8 %collective-permute-start.2 = (s32[2,4,8]{2,1,0:T(4,128)S(1)}, s32[2,4,8]{2,1,0:T(4,128)S(1)}, u32[]{:S(2)}, u32[]{:S(2)}) collective-permute-start(s32[2,4,8]{2,1,0:T(4,128)S(1)} %shard_map.56), channel_id=1, source_target_pairs={{0,2},{1,127},{2,4},{3,1},{4,6},{5,3},{6,8},{7,5},{8,10},{9,7},{10... | collective-permute-start | bytes 776 | tf_op jit(solution)/shard_map/ppermute | solution.py:34
  15.1 9.6 %collective-permute-start.4 = (f32[2,3,8,480]{3,2,1,0:T(8,128)S(1)}, f32[2,3,8,480]{3,2,1,0:T(8,128)S(1)}, u32[]{:S(2)}, u32[]{:S(2)}) collective-permute-start(f32[2,3,8,480]{3,2,1,0:T(8,128)S(1)} %get-tuple-element.14), channel_id=1, source_target_pairs={{0,126},{1,3},{2,0},{3,5},{4,2},{5,7},{6,4},{7,9},{8,6},{9,11},{10... | collective-permute-start | bytes 276488 | tf_op jit(solution)/shard_map/ppermute | solution.py:34
  15.2 10.7 %collective-permute-start.5 = (f32[3,3,4,480]{3,2,1,0:T(4,128)S(1)}, f32[3,3,4,480]{3,2,1,0:T(4,128)S(1)}, u32[]{:S(2)}, u32[]{:S(2)}) collective-permute-start(f32[3,3,4,480]{3,2,1,0:T(4,128)S(1)} %get-tuple-element.15), channel_id=1, source_target_pairs={{0,124},{1,5},{2,126},{3,7},{4,0},{5,9},{6,2},{7,11},{8,4},{9,13},... | collective-permute-start | bytes 207368 | tf_op jit(solution)/shard_map/ppermute | solution.py:34
  24.7 2.6 %collective-permute-start.6 = (f32[2,3,8,480]{3,2,1,0:T(8,128)S(1)}, f32[2,3,8,480]{3,2,1,0:T(8,128)S(1)}, u32[]{:S(2)}, u32[]{:S(2)}) collective-permute-start(f32[2,3,8,480]{3,2,1,0:T(8,128)S(1)} %collective-permute-done.4.refs_0_), channel_id=1, source_target_pairs={{0,1},{1,0},{2,3},{3,2},{4,5},{5,4},{6,7},{7,6},{8,9},{9,8},{10,11... | collective-permute-start | bytes 276488 | tf_op jit(solution)/shard_map/ppermute | solution.py:34
  25.9 1.4 %collective-permute-start.7 = (f32[3,3,4,480]{3,2,1,0:T(4,128)S(1)}, f32[3,3,4,480]{3,2,1,0:T(4,128)S(1)}, u32[]{:S(2)}, u32[]{:S(2)}) collective-permute-start(f32[3,3,4,480]{3,2,1,0:T(4,128)S(1)} %collective-permute-done.5.refs_1_), channel_id=1, source_target_pairs={{0,1},{1,0},{2,3},{3,2},{4,5},{5,4},{6,7},{7,6},{8,9},{9,8},{10,11... | collective-permute-start | bytes 207368 | tf_op jit(solution)/shard_map/ppermute | solution.py:34
  29.1 2.0 %collective-permute-start.8 = (f32[3,64,512]{2,1,0:T(8,128)S(1)}, f32[3,64,512]{2,1,0:T(8,128)S(1)}, u32[]{:S(2)}, u32[]{:S(2)}) collective-permute-start(f32[3,64,512]{2,1,0:T(8,128)S(1)} %shard_map.60.refs_4_.tracers), channel_id=1, source_target_pairs={{0,1},{1,0},{2,3},{3,2},{4,5},{5,4},{6,7},{7,6},{8,9},{9,8},{10,11... | collective-permute-start | bytes 1179656 | tf_op jit(solution)/shard_map/ppermute | solution.py:34
  31.4 9.7 %collective-permute-start.9 = (f32[2,3,8,512]{3,2,1,0:T(8,128)S(1)}, f32[2,3,8,512]{3,2,1,0:T(8,128)S(1)}, u32[]{:S(2)}, u32[]{:S(2)}) collective-permute-start(f32[2,3,8,512]{3,2,1,0:T(8,128)S(1)} %get-tuple-element.20), channel_id=1, source_target_pairs={{0,126},{1,3},{2,0},{3,5},{4,2},{5,7},{6,4},{7,9},{8,6},{9,11},{10... | collective-permute-start | bytes 294920 | tf_op jit(solution)/shard_map/ppermute | solution.py:34
  31.5 9.7 %collective-permute-start.10 = (f32[3,3,4,512]{3,2,1,0:T(4,128)S(1)}, f32[3,3,4,512]{3,2,1,0:T(4,128)S(1)}, u32[]{:S(2)}, u32[]{:S(2)}) collective-permute-start(f32[3,3,4,512]{3,2,1,0:T(4,128)S(1)} %get-tuple-element.21), channel_id=1, source_target_pairs={{0,124},{1,5},{2,126},{3,7},{4,0},{5,9},{6,2},{7,11},{8,4},{9,13},... | collective-permute-start | bytes 221192 | tf_op jit(solution)/shard_map/ppermute | solution.py:34
  41.2 1.4 %collective-permute-start.11 = (f32[2,3,8,512]{3,2,1,0:T(8,128)S(1)}, f32[2,3,8,512]{3,2,1,0:T(8,128)S(1)}, u32[]{:S(2)}, u32[]{:S(2)}) collective-permute-start(f32[2,3,8,512]{3,2,1,0:T(8,128)S(1)} %collective-permute-done.9.refs_0_), channel_id=1, source_target_pairs={{0,1},{1,0},{2,3},{3,2},{4,5},{5,4},{6,7},{7,6},{8,9},{9,8},{10,11... | collective-permute-start | bytes 294920 | tf_op jit(solution)/shard_map/ppermute | solution.py:34
  41.2 1.4 %collective-permute-start.12 = (f32[3,3,4,512]{3,2,1,0:T(4,128)S(1)}, f32[3,3,4,512]{3,2,1,0:T(4,128)S(1)}, u32[]{:S(2)}, u32[]{:S(2)}) collective-permute-start(f32[3,3,4,512]{3,2,1,0:T(4,128)S(1)} %collective-permute-done.10.refs_1_), channel_id=1, source_target_pairs={{0,1},{1,0},{2,3},{3,2},{4,5},{5,4},{6,7},{7,6},{8,9},{9,8},{10,11... | collective-permute-start | bytes 221192 | tf_op jit(solution)/shard_map/ppermute | solution.py:34

commit v2 on v1

--- a/solution.py
+++ b/solution.py
@@ -86,29 +86,63 @@
             turned[step, level] = both.T
 
 
+def chosen(core, groups, sources):
+    lane = lax.broadcasted_iota(jnp.int32, (CAP, ELEMS), 1)
+    rows = []
+    for source, low, high in groups:
+        lists = sources[source]
+        wanted = jnp.where(core == 0, lists[:, low:low + 1], lists[:, high:high + 1])
+        rows.append((jnp.broadcast_to(wanted, (CAP, ELEMS)) == lane).astype(f32))
+    return jnp.concatenate(rows, axis=0).astype(bf16)
+
+
+def picked(picks, rows):
+    high, rest = split(rows)
+    middle, low = split(rest)
+    parts = jnp.concatenate([high.astype(bf16), middle.astype(bf16), low.astype(bf16)], axis=0)
+    return jnp.dot(jnp.concatenate([picks, picks, picks], axis=1), parts, preferred_element_type=f32)
+
+
+def lay(level, mine, lent, near, far, inner):
+    for i in range(2):
+        near[i, level, 0:CAP] = mine[i * CAP:(i + 1) * CAP]
+        near[i, level, CAP:2 * CAP] = lent[i * CAP:(i + 1) * CAP]
+        far[i, level] = mine[(2 + i) * CAP:(3 + i) * CAP]
+    far[2, level] = lent[2 * CAP:3 * CAP]
+    inner[level] = lent[3 * CAP:4 * CAP]
+
+
 def pack(me, asked2, asked1, lists, own, other, near, far, inner):
-    lane = lax.broadcasted_iota(jnp.int32, (CAP, LANES), 1)
     sources = [asked1.at[0], asked1.at[1], asked2.at[0], asked2.at[1], lists]
-    picks = []
-    for source, first, second in PACKED:
-        one = [sources[source][:, j:j + 1] + ELEMS * place for j, place in (first, second)]
-        picks.append((jnp.broadcast_to(jnp.where(me[0] == 0, one[0], one[1]), (CAP, LANES)) == lane).astype(f32))
-    picks = jnp.concatenate(picks, axis=0).astype(bf16)
-    picks = jnp.concatenate([picks, picks, picks], axis=1)
-    for level in range(LEV):
-        high, rest = split(jnp.concatenate([own[level], other[level]], axis=0))
-        middle, low = split(rest)
-        parts = jnp.concatenate([high.astype(bf16), middle.astype(bf16), low.astype(bf16)], axis=0)
-        rows = jnp.dot(picks, parts, preferred_element_type=f32)
-        near[0, level] = rows[0:8]
-        near[1, level] = rows[8:16]
-        for g in range(3):
-            far[g, level] = rows[16 + 4 * g:20 + 4 * g]
-        inner[level] = rows[28:32]
-
-
-def substep(step, near, far, near_other, far_other, inner, table, hot, turned, out, whole, mixed, close, spaced, rowed, done):
+    none = jnp.zeros((4 * CAP, ELEMS), bf16)
+    picks = jnp.concatenate([jnp.concatenate([chosen(me[0], OWN, sources), none], axis=1),
+                             jnp.concatenate([none, chosen(me[0], LENT, sources)], axis=1)], axis=0)
+    for level in range(LEV):
+        rows = picked(picks, jnp.concatenate([own[level], other[level]], axis=0))
+        lay(level, rows[0:4 * CAP], rows[4 * CAP:8 * CAP], near, far, inner)
+
+
+def choose(me, asked2, asked1, lists2, lists1, lists, picks):
+    both = [chosen(me[0], OWN, [asked1.at[0], asked1.at[1], asked2.at[0], asked2.at[1]]),
+            chosen(1 - me[0], LENT, [lists1.at[0], lists1.at[1], lists2.at[0], lists2.at[1], lists])]
+    picks[...] = jnp.concatenate(both, axis=0)
+
+
+def pick(picks, rows, mine, lent):
+    for level in range(LEV):
+        both = picked(picks[...], rows[level])
+        mine[level] = both[0:4 * CAP]
+        lent[level] = both[4 * CAP:8 * CAP]
+
+
+def merge(mine, lent, near, far, inner):
+    for level in range(LEV):
+        lay(level, mine[level], lent[level], near, far, inner)
+
+
+def substep(step, near, far, near_other, far_other, inner, table, hot, turned, *refs):
     last = step + 1 == SUBSTEPS
+    out, whole, mixed, close, spaced, rowed, done = refs
     half = 8 * TRACERS
     spaced[:, ROW:, :] = jnp.zeros_like(spaced[:, ROW:, :])
 
@@ -176,11 +210,9 @@
 
 
 TABLE = shaped(LEV, TALL, 2 * ELEMS, dtype=bf16)
-HELD = ((5, 6, 7, 2, 3, 0, 1, 4), (1, 2, 0, 4, 5, 6, 7, 3))
-PACKED = (
-    (0, (5, 0), (1, 1)), (0, (6, 1), (2, 0)), (1, (4, 0), (2, 1)), (1, (5, 1), (3, 0)),
-    (2, (7, 0), (0, 0)), (3, (6, 0), (0, 1)), (3, (7, 1), (1, 0)), (4, (4, 1), (3, 1)),
-)
+HELD = ((5, 6, 7, 3, 2, 1, 0, 4), (2, 1, 0, 4, 5, 6, 7, 3))
+OWN = ((0, 5, 2), (1, 4, 3), (2, 7, 0), (3, 6, 1))
+LENT = ((0, 6, 1), (1, 5, 2), (3, 7, 0), (4, 4, 3))
 SCRATCH = [
     pltpu.VMEM((LEV, TALL, DEPTH), bf16),
     pltpu.VMEM((LEV, 8 * WIDE, LANES), f32),
@@ -234,10 +266,11 @@
     for step in range(SUBSTEPS):
         last = step + 1 == SUBSTEPS
         width = TALL if step else ROW
-        near, far, inner = call(
-            lambda *refs: pack(*refs), [me] + asked + [levels, other],
-            (shaped(2, LEV, 2 * CAP, width), shaped(3, LEV, CAP, width), shaped(LEV, CAP, width)),
-            smem=(0,))
+        pieces = (shaped(2, LEV, 2 * CAP, width), shaped(3, LEV, CAP, width), shaped(LEV, CAP, width))
+        if step:
+            near, far, inner = call(merge, [mine, lent], pieces)
+        else:
+            near, far, inner = call(pack, [me] + asked + [levels, other], pieces, smem=(0,))
         far = kept(ahead(far, -2))
         near = kept(ahead(near, -1))
         inner = kept(inner)
@@ -253,13 +286,20 @@
                  pltpu.SemaphoreType.DMA((3,))], smem=(0,), outside=(2, 3, 4)))
         far_other = kept(swapped(far))
         near_other = kept(swapped(near))
+        if not last:
+            their2 = kept(swapped(asked2))
+            their1 = kept(swapped(asked1))
+            picks = kept(call(choose, [me, asked2, asked1, their2, their1, partner_lists],
+                              shaped(8 * CAP, ELEMS, dtype=bf16), smem=(0,)))
         levels = call(
             lambda *refs: substep(step, *refs),
             [near, far, near_other, far_other, inner, table, hot, turned],
-            shaped(LEV, ELEMS, ROW if last else TALL), SCRATCH, keep=not last)
+            shaped(LEV, ELEMS, ROW if last else TALL), SCRATCH,
+            keep=not last)
         if not last:
             levels = kept(levels)
-            other = kept(swapped(levels))
+            mine, lent = map(kept, call(pick, [picks, levels], (shaped(LEV, 4 * CAP, TALL),) * 2))
+            lent = kept(swapped(lent))
     return jnp.transpose(levels, (1, 0, 2))
 
 

time: 45.1 us -> 46.4 us (1.029)
  waiting for transfers between devices: 24.2 us -> 25.4 us
    ppermute x13 -> x15, waiting for transfers between devices: 24.2 us -> 25.4 us  [moved(): lax.ppermute(value, 'sfc', [(source, target(source) % N) for source in ra...]
    ppermute x13 -> x15, starting transfers between devices: 12.5 us -> 12.4 us  [moved(): lax.ppermute(value, 'sfc', [(source, target(source) % N) for source in ra...]
    pallas_call x9 -> x11, Pallas kernels: 8.19 us -> 8.26 us  [call(): pl.pallas_call(body, in_specs=[SMEM if i in smem else HBM if i in outside...]
  transfers between devices with their start and end apart: 13 -> 15, of which waited for: 6 -> 6; matrix products, arithmetic and copies ran while one was open for 0% -> 0% of each run, Pallas kernels for 7% -> 7%
where the time goes in v2:
time: 46.4 us; the launch traced here: 46.2 us
  waiting for transfers between devices  25.4 us (55%)
  starting transfers between devices  12.4 us (27%)
  Pallas kernels  8.26 us (18%)
    ppermute x15, waiting for transfers between devices, moved(): lax.ppermute(value, 'sfc', [(source, target(source) % N) for source in ra...  25.4 us
    ppermute x15, starting transfers between devices, moved(): lax.ppermute(value, 'sfc', [(source, target(source) % N) for source in ra...  12.4 us
    pallas_call x11, Pallas kernels, call(): pl.pallas_call(body, in_specs=[SMEM if i in smem else HBM if i in outside...  8.26 us
  transfers between devices with their start and end apart: 15, of which 6 were waited for; matrix products, arithmetic and copies ran while one was open for 0% of the time, Pallas kernels for 7%

profile of v2, /device:TPU:1, one launch (start us, length us, event | category | flops | bytes accessed | tf_op | source)
XLA Modules:
  0.0 46.2 jit_solution(983483202651821461)
XLA Ops:
  0.0 1.4 %collective-permute-start.5 = (f32[3,64,480]{2,1,0:T(8,128)}, f32[3,64,480]{2,1,0:T(8,128)S(1)}, u32[]{:S(2)}, u32[]{:S(2)}) collective-permute-start(f32[3,64,480]{2,1,0:T(8,128)} %bitcast.8), channel_id=1, source_target_pairs={{0,1},{1,0},{2,3},{3,2},{4,5},{5,4},{6,7},{7,6},{8,9},{9,8},{10,11... | collective-permute-start | bytes 1105928 | tf_op jit(solution)/shard_map/ppermute | solution.py:34
  1.4 0.0 collective-permute-start
  1.4 0.7 %shard_map.55.mine.lists = s32[4,8]{1,0:T(4,128)S(1)} custom-call(s32[4,8]{1,0:T(4,128)} %bitcast.13), custom_call_target="tpu_custom_call" | custom-call | tf_op jit(solution)/shard_map/pallas_call | solution.py:243
  2.1 1.0 %shard_map.58.own.tracers = f32[3,64,480]{2,1,0:T(8,128)S(1)} custom-call(f32[3,64,480]{2,1,0:T(8,128)} %bitcast.9), custom_call_target="tpu_custom_call" | custom-call | tf_op jit(solution)/shard_map/pallas_call | solution.py:243
  3.1 0.0 collective-permute-done.theirs.lists
  3.1 8.6 %collective-permute-start.2 = (s32[2,4,8]{2,1,0:T(4,128)S(1)}, s32[2,4,8]{2,1,0:T(4,128)S(1)}, u32[]{:S(2)}, u32[]{:S(2)}) collective-permute-start(s32[2,4,8]{2,1,0:T(4,128)S(1)} %shard_map.56), channel_id=1, source_target_pairs={{0,2},{1,127},{2,4},{3,1},{4,6},{5,3},{6,8},{7,5},{8,10},{9,7},{10... | collective-permute-start | bytes 776 | tf_op jit(solution)/shard_map/ppermute | solution.py:34
  11.7 0.5 %collective-permute-start.1 = (s32[2,4,8]{2,1,0:T(4,128)S(1)}, s32[2,4,8]{2,1,0:T(4,128)S(1)}, u32[]{:S(2)}, u32[]{:S(2)}) collective-permute-start(s32[2,4,8]{2,1,0:T(4,128)S(1)} %shard_map.56), channel_id=1, source_target_pairs={{0,4},{1,125},{2,6},{3,127},{4,8},{5,1},{6,10},{7,3},{8,12},{9,5},... | collective-permute-start | bytes 776 | tf_op jit(solution)/shard_map/ppermute | solution.py:34
  12.2 0.2 collective-permute-done.2.asked1
  12.5 3.3 %collective-permute-done.1.asked2 = s32[2,4,8]{2,1,0:T(4,128)S(1)} collective-permute-done((s32[2,4,8]{2,1,0:T(4,128)S(1)}, s32[2,4,8]{2,1,0:T(4,128)S(1)}, u32[]{:S(2)}, u32[]{:S(2)}) %collective-permute-start.1) | collective-permute-done | bytes 288 | tf_op jit(solution)/shard_map/ppermute | solution.py:34
  15.8 0.0 collective-permute-done.5.other
  15.8 0.5 %shard_map.59 = (f32[2,3,8,480]{3,2,1,0:T(8,128)S(1)}, f32[3,3,4,480]{3,2,1,0:T(4,128)S(1)}, f32[3,4,480]{2,1,0:T(4,128)S(1)}) custom-call(s32[1]{0:T(128)S(6)} %select_n.7.me, s32[2,4,8]{2,1,0:T(4,128)S(1)} %collective-permute-done.1.asked2, s32[2,4,8]{2,1,0:T(4,128)S(1)} %collective-permute-done.2.asked1, s32[4,8]{1,0:T(4,128)S(1)} %shard_map.55.mine.lists, ...), custom_call_target="tpu_custom_call" | custom-call | tf_op jit(solution)/shard_map/pallas_call | solution.py:243
  16.2 0.0 collective-permute-start.6
  16.3 0.1 collective-permute-start.7
  16.4 10.3 %collective-permute-done.6.refs_0_ = f32[2,3,8,480]{3,2,1,0:T(8,128)S(1)} collective-permute-done((f32[2,3,8,480]{3,2,1,0:T(8,128)S(1)}, f32[2,3,8,480]{3,2,1,0:T(8,128)S(1)}, u32[]{:S(2)}, u32[]{:S(2)}) %collective-permute-start.6) | collective-permute-done | bytes 92192 | tf_op jit(solution)/shard_map/ppermute | solution.py:34
  26.6 0.0 collective-permute-start.8
  26.6 0.0 collective-permute-done.7.refs_1_
  26.6 0.5 %collective-permute-start.9 = (f32[3,3,4,480]{3,2,1,0:T(4,128)S(1)}, f32[3,3,4,480]{3,2,1,0:T(4,128)S(1)}, u32[]{:S(2)}, u32[]{:S(2)}) collective-permute-start(f32[3,3,4,480]{3,2,1,0:T(4,128)S(1)} %collective-permute-done.7.refs_1_), channel_id=1, source_target_pairs={{0,1},{1,0},{2,3},{3,2},{4,5},{5,4},{6,7},{7,6},{8,9},{9,8},{10,11... | collective-permute-start | bytes 207368 | tf_op jit(solution)/shard_map/ppermute | solution.py:34
  27.2 0.0 collective-permute-start.4
  27.2 0.5 %collective-permute-start.3 = (s32[2,4,8]{2,1,0:T(4,128)S(1)}, s32[2,4,8]{2,1,0:T(4,128)S(1)}, u32[]{:S(2)}, u32[]{:S(2)}) collective-permute-start(s32[2,4,8]{2,1,0:T(4,128)S(1)} %collective-permute-done.1.asked2), channel_id=1, source_target_pairs={{0,1},{1,0},{2,3},{3,2},{4,5},{5,4},{6,7},{7,6},{8,9},{9,8},{10,11... | collective-permute-start | bytes 776 | tf_op jit(solution)/shard_map/ppermute | solution.py:34
  27.7 1.4 %shard_map.60 = (bf16[3,512,128]{2,1,0:T(8,128)(2,1)S(1)}, bf16[3,4,192,256]{3,2,1,0:T(8,128)(2,1)S(1)}, f32[2,3,128,128]{3,2,1,0:T(8,128)S(1)}) custom-call(s32[1]{0:T(128)S(6)} %select_n.7.me, f32[3,64,480]{2,1,0:T(8,128)S(1)} %shard_map.58.own.tracers, s32[1,8]{1,0:T(1,128)} %counts_in.1, f32[2,3,64,256]{3,2,1,0:T(8,128)} %bitcast.10, s32[48,64]{1,0:T(8,128)} %bitcast.11), custom_call_target="tpu_custom_call" | custom-call | tf_op jit(solution)/shard_map/pallas_call | solution.py:243
  29.1 0.0 collective-permute-done.4.lists1
  29.1 0.0 collective-permute-done.3.lists2
  29.1 0.2 shard_map.57.picks
  29.3 0.0 collective-permute-done.9.refs_3_
  29.3 0.0 collective-permute-done.8.refs_2_
  29.3 1.7 %shard_map.61.rows.tracers = f32[3,64,512]{2,1,0:T(8,128)S(1)} custom-call(f32[2,3,8,480]{3,2,1,0:T(8,128)S(1)} %collective-permute-done.6.refs_0_, f32[3,3,4,480]{3,2,1,0:T(4,128)S(1)} %collective-permute-done.7.refs_1_, f32[2,3,8,480]{3,2,1,0:T(8,128)S(1)} %collective-permute-done.8.refs_2_, f32[3,3,4,480]{3,2,1,0:T(4,128)S(1)} %collective-permute-done.9.refs_3_, ...), custom_call_target="tpu_custom_call" | custom-call | tf_op jit(solution)/shard_map/pallas_call | solution.py:243
  31.0 0.3 shard_map.62
  31.3 0.1 collective-permute-start.10
  31.3 1.3 %collective-permute-done.10.lent = f32[3,16,512]{2,1,0:T(8,128)S(1)} collective-permute-done((f32[3,16,512]{2,1,0:T(8,128)S(1)}, f32[3,16,512]{2,1,0:T(8,128)S(1)}, u32[]{:S(2)}, u32[]{:S(2)}) %collective-permute-start.10) | collective-permute-done | bytes 98336 | tf_op jit(solution)/shard_map/ppermute | solution.py:34
  32.6 0.1 collective-permute-start.11
  32.7 0.1 collective-permute-start.12
  32.8 9.6 %collective-permute-done.11.refs_0_ = f32[2,3,8,512]{3,2,1,0:T(8,128)S(1)} collective-permute-done((f32[2,3,8,512]{3,2,1,0:T(8,128)S(1)}, f32[2,3,8,512]{3,2,1,0:T(8,128)S(1)}, u32[]{:S(2)}, u32[]{:S(2)}) %collective-permute-start.11) | collective-permute-done | bytes 98336 | tf_op jit(solution)/shard_map/ppermute | solution.py:34
  42.4 0.0 collective-permute-start.13
  42.4 0.0 collective-permute-done.12.refs_1_
  42.4 0.5 %collective-permute-start.14 = (f32[3,3,4,512]{3,2,1,0:T(4,128)S(1)}, f32[3,3,4,512]{3,2,1,0:T(4,128)S(1)}, u32[]{:S(2)}, u32[]{:S(2)}) collective-permute-start(f32[3,3,4,512]{3,2,1,0:T(4,128)S(1)} %collective-permute-done.12.refs_1_), channel_id=1, source_target_pairs={{0,1},{1,0},{2,3},{3,2},{4,5},{5,4},{6,7},{7,6},{8,9},{9,8},{10,11... | collective-permute-start | bytes 221192 | tf_op jit(solution)/shard_map/ppermute | solution.py:34
  42.9 0.2 shard_map.64.refs_5_
  43.1 0.7 %collective-permute-done.14.refs_3_ = f32[3,3,4,512]{3,2,1,0:T(4,128)S(1)} collective-permute-done((f32[3,3,4,512]{3,2,1,0:T(4,128)S(1)}, f32[3,3,4,512]{3,2,1,0:T(4,128)S(1)}, u32[]{:S(2)}, u32[]{:S(2)}) %collective-permute-start.14) | collective-permute-done | bytes 73760 | tf_op jit(solution)/shard_map/ppermute | solution.py:34
  43.8 0.0 collective-permute-done.13.refs_2_
  43.8 2.4 %shard_map.65 = f32[3,64,480]{2,1,0:T(8,128)} custom-call(f32[2,3,8,512]{3,2,1,0:T(8,128)S(1)} %collective-permute-done.11.refs_0_, f32[3,3,4,512]{3,2,1,0:T(4,128)S(1)} %collective-permute-done.12.refs_1_, f32[2,3,8,512]{3,2,1,0:T(8,128)S(1)} %collective-permute-done.13.refs_2_, f32[3,3,4,512]{3,2,1,0:T(4,128)S(1)} %collective-permute-done.14.refs_3_, ...), custom_call_target="tpu_custom_call" | custom-call | tf_op jit(solution)/shard_map/pallas_call | solution.py:243
  (2 shorter events, 0.0 us)
Async XLA Ops:
  0.0 15.8 %collective-permute-start.5 = (f32[3,64,480]{2,1,0:T(8,128)}, f32[3,64,480]{2,1,0:T(8,128)S(1)}, u32[]{:S(2)}, u32[]{:S(2)}) collective-permute-start(f32[3,64,480]{2,1,0:T(8,128)} %bitcast.8), channel_id=1, source_target_pairs={{0,1},{1,0},{2,3},{3,2},{4,5},{5,4},{6,7},{7,6},{8,9},{9,8},{10,11... | collective-permute-start | bytes 1105928 | tf_op jit(solution)/shard_map/ppermute | solution.py:34
  1.4 1.7 %collective-permute-start = (s32[4,8]{1,0:T(4,128)}, s32[4,8]{1,0:T(4,128)S(1)}, u32[]{:S(2)}, u32[]{:S(2)}) collective-permute-start(s32[4,8]{1,0:T(4,128)} %bitcast.12), channel_id=1, source_target_pairs={{0,1},{1,0},{2,3},{3,2},{4,5},{5,4},{6,7},{7,6},{8,9},{9,8},{10,11... | collective-permute-start | bytes 392 | tf_op jit(solution)/shard_map/ppermute | solution.py:34
  3.1 9.3 %collective-permute-start.2 = (s32[2,4,8]{2,1,0:T(4,128)S(1)}, s32[2,4,8]{2,1,0:T(4,128)S(1)}, u32[]{:S(2)}, u32[]{:S(2)}) collective-permute-start(s32[2,4,8]{2,1,0:T(4,128)S(1)} %shard_map.56), channel_id=1, source_target_pairs={{0,2},{1,127},{2,4},{3,1},{4,6},{5,3},{6,8},{7,5},{8,10},{9,7},{10... | collective-permute-start | bytes 776 | tf_op jit(solution)/shard_map/ppermute | solution.py:34
  11.7 4.1 %collective-permute-start.1 = (s32[2,4,8]{2,1,0:T(4,128)S(1)}, s32[2,4,8]{2,1,0:T(4,128)S(1)}, u32[]{:S(2)}, u32[]{:S(2)}) collective-permute-start(s32[2,4,8]{2,1,0:T(4,128)S(1)} %shard_map.56), channel_id=1, source_target_pairs={{0,4},{1,125},{2,6},{3,127},{4,8},{5,1},{6,10},{7,3},{8,12},{9,5},... | collective-permute-start | bytes 776 | tf_op jit(solution)/shard_map/ppermute | solution.py:34
  16.2 10.4 %collective-permute-start.6 = (f32[2,3,8,480]{3,2,1,0:T(8,128)S(1)}, f32[2,3,8,480]{3,2,1,0:T(8,128)S(1)}, u32[]{:S(2)}, u32[]{:S(2)}) collective-permute-start(f32[2,3,8,480]{3,2,1,0:T(8,128)S(1)} %get-tuple-element.16), channel_id=1, source_target_pairs={{0,126},{1,3},{2,0},{3,5},{4,2},{5,7},{6,4},{7,9},{8,6},{9,11},{10... | collective-permute-start | bytes 276488 | tf_op jit(solution)/shard_map/ppermute | solution.py:34
  16.3 10.3 %collective-permute-start.7 = (f32[3,3,4,480]{3,2,1,0:T(4,128)S(1)}, f32[3,3,4,480]{3,2,1,0:T(4,128)S(1)}, u32[]{:S(2)}, u32[]{:S(2)}) collective-permute-start(f32[3,3,4,480]{3,2,1,0:T(4,128)S(1)} %get-tuple-element.17), channel_id=1, source_target_pairs={{0,124},{1,5},{2,126},{3,7},{4,0},{5,9},{6,2},{7,11},{8,4},{9,13},... | collective-permute-start | bytes 207368 | tf_op jit(solution)/shard_map/ppermute | solution.py:34
  26.6 2.7 %collective-permute-start.8 = (f32[2,3,8,480]{3,2,1,0:T(8,128)S(1)}, f32[2,3,8,480]{3,2,1,0:T(8,128)S(1)}, u32[]{:S(2)}, u32[]{:S(2)}) collective-permute-start(f32[2,3,8,480]{3,2,1,0:T(8,128)S(1)} %collective-permute-done.6.refs_0_), channel_id=1, source_target_pairs={{0,1},{1,0},{2,3},{3,2},{4,5},{5,4},{6,7},{7,6},{8,9},{9,8},{10,11... | collective-permute-start | bytes 276488 | tf_op jit(solution)/shard_map/ppermute | solution.py:34
  26.6 2.6 %collective-permute-start.9 = (f32[3,3,4,480]{3,2,1,0:T(4,128)S(1)}, f32[3,3,4,480]{3,2,1,0:T(4,128)S(1)}, u32[]{:S(2)}, u32[]{:S(2)}) collective-permute-start(f32[3,3,4,480]{3,2,1,0:T(4,128)S(1)} %collective-permute-done.7.refs_1_), channel_id=1, source_target_pairs={{0,1},{1,0},{2,3},{3,2},{4,5},{5,4},{6,7},{7,6},{8,9},{9,8},{10,11... | collective-permute-start | bytes 207368 | tf_op jit(solution)/shard_map/ppermute | solution.py:34
  27.2 1.9 %collective-permute-start.4 = (s32[2,4,8]{2,1,0:T(4,128)S(1)}, s32[2,4,8]{2,1,0:T(4,128)S(1)}, u32[]{:S(2)}, u32[]{:S(2)}) collective-permute-start(s32[2,4,8]{2,1,0:T(4,128)S(1)} %collective-permute-done.2.asked1), channel_id=1, source_target_pairs={{0,1},{1,0},{2,3},{3,2},{4,5},{5,4},{6,7},{7,6},{8,9},{9,8},{10,11... | collective-permute-start | bytes 776 | tf_op jit(solution)/shard_map/ppermute | solution.py:34
  27.2 2.0 %collective-permute-start.3 = (s32[2,4,8]{2,1,0:T(4,128)S(1)}, s32[2,4,8]{2,1,0:T(4,128)S(1)}, u32[]{:S(2)}, u32[]{:S(2)}) collective-permute-start(s32[2,4,8]{2,1,0:T(4,128)S(1)} %collective-permute-done.1.asked2), channel_id=1, source_target_pairs={{0,1},{1,0},{2,3},{3,2},{4,5},{5,4},{6,7},{7,6},{8,9},{9,8},{10,11... | collective-permute-start | bytes 776 | tf_op jit(solution)/shard_map/ppermute | solution.py:34
  31.3 1.4 %collective-permute-start.10 = (f32[3,16,512]{2,1,0:T(8,128)S(1)}, f32[3,16,512]{2,1,0:T(8,128)S(1)}, u32[]{:S(2)}, u32[]{:S(2)}) collective-permute-start(f32[3,16,512]{2,1,0:T(8,128)S(1)} %get-tuple-element.23), channel_id=1, source_target_pairs={{0,1},{1,0},{2,3},{3,2},{4,5},{5,4},{6,7},{7,6},{8,9},{9,8},{10,11... | collective-permute-start | bytes 294920 | tf_op jit(solution)/shard_map/ppermute | solution.py:34
  32.6 9.8 %collective-permute-start.11 = (f32[2,3,8,512]{3,2,1,0:T(8,128)S(1)}, f32[2,3,8,512]{3,2,1,0:T(8,128)S(1)}, u32[]{:S(2)}, u32[]{:S(2)}) collective-permute-start(f32[2,3,8,512]{3,2,1,0:T(8,128)S(1)} %get-tuple-element.24), channel_id=1, source_target_pairs={{0,126},{1,3},{2,0},{3,5},{4,2},{5,7},{6,4},{7,9},{8,6},{9,11},{10... | collective-permute-start | bytes 294920 | tf_op jit(solution)/shard_map/ppermute | solution.py:34
  32.7 9.7 %collective-permute-start.12 = (f32[3,3,4,512]{3,2,1,0:T(4,128)S(1)}, f32[3,3,4,512]{3,2,1,0:T(4,128)S(1)}, u32[]{:S(2)}, u32[]{:S(2)}) collective-permute-start(f32[3,3,4,512]{3,2,1,0:T(4,128)S(1)} %get-tuple-element.25), channel_id=1, source_target_pairs={{0,124},{1,5},{2,126},{3,7},{4,0},{5,9},{6,2},{7,11},{8,4},{9,13},... | collective-permute-start | bytes 221192 | tf_op jit(solution)/shard_map/ppermute | solution.py:34
  42.4 1.4 %collective-permute-start.13 = (f32[2,3,8,512]{3,2,1,0:T(8,128)S(1)}, f32[2,3,8,512]{3,2,1,0:T(8,128)S(1)}, u32[]{:S(2)}, u32[]{:S(2)}) collective-permute-start(f32[2,3,8,512]{3,2,1,0:T(8,128)S(1)} %collective-permute-done.11.refs_0_), channel_id=1, source_target_pairs={{0,1},{1,0},{2,3},{3,2},{4,5},{5,4},{6,7},{7,6},{8,9},{9,8},{10,11... | collective-permute-start | bytes 294920 | tf_op jit(solution)/shard_map/ppermute | solution.py:34
  42.4 1.4 %collective-permute-start.14 = (f32[3,3,4,512]{3,2,1,0:T(4,128)S(1)}, f32[3,3,4,512]{3,2,1,0:T(4,128)S(1)}, u32[]{:S(2)}, u32[]{:S(2)}) collective-permute-start(f32[3,3,4,512]{3,2,1,0:T(4,128)S(1)} %collective-permute-done.12.refs_1_), channel_id=1, source_target_pairs={{0,1},{1,0},{2,3},{3,2},{4,5},{5,4},{6,7},{7,6},{8,9},{9,8},{10,11... | collective-permute-start | bytes 221192 | tf_op jit(solution)/shard_map/ppermute | solution.py:34

commit v3 on v2

--- a/solution.py
+++ b/solution.py
@@ -21,6 +21,7 @@
 PAIRS = 4
 LANES = 128
 N = 128
+PLANE = 16
 
 
 VMEM = pl.BlockSpec(memory_space=pltpu.VMEM)
@@ -40,6 +41,20 @@
 
 def ahead(value, chips):
     return moved(value, lambda device: device + 2 * chips * (1 - 2 * (device % 2)))
+
+
+def stepped(value):
+    return moved(value, lambda device: device - 2 * PLANE if device % 2 and device // 2 % PLANE < 2 else device)
+
+
+def asking(value, chips):
+    def target(device):
+        chip = device // 2
+        if device % 2 == 0:
+            return device + 2 * chips
+        return 2 * (chip // PLANE * PLANE + (chip - chips) % PLANE) + 1
+
+    return moved(value, target)
 
 
 def split(x):
@@ -232,6 +247,10 @@
     both[1] = theirs[...]
 
 
+def first_leg(place, both, moved_lists, out):
+    out[...] = jnp.where(place[0] == 1, moved_lists[...], both[...])
+
+
 def fetch(source, target, done):
     copy = pltpu.make_async_copy(source, target, done)
     copy.start()
@@ -252,6 +271,7 @@
 
 def on_device(tracers, weights, departure, needs, counts):
     me = lax.axis_index("sfc")[None] % 2
+    place = lax.axis_index("sfc")[None] % (2 * PLANE)
     levels = jnp.transpose(tracers, (1, 0, 2))
     lists = jnp.transpose(needs[0], (1, 0))
     partner_lists = kept(swapped(lists))
@@ -259,8 +279,10 @@
     lists = kept(call(fetch, [lists], shaped(CAP, 2 * REACH, dtype=jnp.int32), [pltpu.SemaphoreType.DMA(())],
                       outside=(0,)))
     both = kept(call(join, [lists, partner_lists], shaped(2, CAP, 2 * REACH, dtype=jnp.int32)))
-    asked2 = kept(ahead(both, 2))
-    asked1 = kept(ahead(both, 1))
+    moved_lists = kept(stepped(both))
+    one = kept(call(first_leg, [place, both, moved_lists], shaped(2, CAP, 2 * REACH, dtype=jnp.int32), smem=(0,)))
+    asked2 = kept(asking(moved_lists, 2))
+    asked1 = kept(asking(one, 1))
     asked = [asked2, asked1, lists]
     levels = kept(call(fetch, [levels], shaped(LEV, ELEMS, ROW), [pltpu.SemaphoreType.DMA(())], outside=(0,)))
     for step in range(SUBSTEPS):

time: 46.4 us -> 46.7 us (level)
  starting transfers between devices: 12.4 us -> 13.9 us
  waiting for transfers between devices: 25.4 us -> 24.2 us
    ppermute x15 -> x16, starting transfers between devices: 12.4 us -> 13.9 us  [moved(): lax.ppermute(value, 'sfc', [(source, target(source) % N) for source in ra...]
    ppermute x15 -> x16, waiting for transfers between devices: 25.4 us -> 24.2 us  [moved(): lax.ppermute(value, 'sfc', [(source, target(source) % N) for source in ra...]
    pallas_call x11 -> x12, Pallas kernels: 8.26 us -> 8.26 us  [call(): pl.pallas_call(body, in_specs=[SMEM if i in smem else HBM if i in outside...]
  transfers between devices with their start and end apart: 15 -> 16, of which waited for: 6 -> 7; matrix products, arithmetic and copies ran while one was open for 0% -> 0% of each run, Pallas kernels for 7% -> 7%
where the time goes in v3:
time: 46.7 us; the launch traced here: 46.5 us
  waiting for transfers between devices  24.2 us (52%)
  starting transfers between devices  13.9 us (30%)
  Pallas kernels  8.26 us (18%)
    ppermute x16, waiting for transfers between devices, moved(): lax.ppermute(value, 'sfc', [(source, target(source) % N) for source in ra...  24.2 us
    ppermute x16, starting transfers between devices, moved(): lax.ppermute(value, 'sfc', [(source, target(source) % N) for source in ra...  13.9 us
    pallas_call x12, Pallas kernels, call(): pl.pallas_call(body, in_specs=[SMEM if i in smem else HBM if i in outside...  8.26 us
  transfers between devices with their start and end apart: 16, of which 7 were waited for; matrix products, arithmetic and copies ran while one was open for 0% of the time, Pallas kernels for 7%

profile of v3, /device:TPU:1, one launch (start us, length us, event | category | flops | bytes accessed | tf_op | source)
XLA Modules:
  0.0 46.5 jit_solution(5607821848645725977)
XLA Ops:
  0.0 1.4 %collective-permute-start.6 = (f32[3,64,480]{2,1,0:T(8,128)}, f32[3,64,480]{2,1,0:T(8,128)S(1)}, u32[]{:S(2)}, u32[]{:S(2)}) collective-permute-start(f32[3,64,480]{2,1,0:T(8,128)} %bitcast.8), channel_id=1, source_target_pairs={{0,1},{1,0},{2,3},{3,2},{4,5},{5,4},{6,7},{7,6},{8,9},{9,8},{10,11... | collective-permute-start | bytes 1105928 | tf_op jit(solution)/shard_map/ppermute | solution.py:35
  1.4 0.0 collective-permute-start
  1.4 0.7 %shard_map.55.mine.lists = s32[4,8]{1,0:T(4,128)S(1)} custom-call(s32[4,8]{1,0:T(4,128)} %bitcast.13), custom_call_target="tpu_custom_call" | custom-call | tf_op jit(solution)/shard_map/pallas_call | solution.py:262
  2.1 0.9 %collective-permute-done.theirs.lists = s32[4,8]{1,0:T(4,128)S(1)} collective-permute-done((s32[4,8]{1,0:T(4,128)}, s32[4,8]{1,0:T(4,128)S(1)}, u32[]{:S(2)}, u32[]{:S(2)}) %collective-permute-start) | collective-permute-done | bytes 160 | tf_op jit(solution)/shard_map/ppermute | solution.py:35
  2.9 4.7 %collective-permute-start.1 = (s32[2,4,8]{2,1,0:T(4,128)S(1)}, s32[2,4,8]{2,1,0:T(4,128)S(1)}, u32[]{:S(2)}, u32[]{:S(2)}) collective-permute-start(s32[2,4,8]{2,1,0:T(4,128)S(1)} %shard_map.56.both), channel_id=1, source_target_pairs={{0,0},{1,97},{2,2},{3,99},{4,4},{5,5},{6,6},{7,7},{8,8},{9,9},{10,... | collective-permute-start | bytes 776 | tf_op jit(solution)/shard_map/ppermute | solution.py:35
  7.7 1.0 %shard_map.59.own.tracers = f32[3,64,480]{2,1,0:T(8,128)S(1)} custom-call(f32[3,64,480]{2,1,0:T(8,128)} %bitcast.9), custom_call_target="tpu_custom_call" | custom-call | tf_op jit(solution)/shard_map/pallas_call | solution.py:262
  8.7 0.0 collective-permute-done.1.moved_lists
  8.7 2.0 %collective-permute-start.3 = (s32[2,4,8]{2,1,0:T(4,128)S(1)}, s32[2,4,8]{2,1,0:T(4,128)S(1)}, u32[]{:S(2)}, u32[]{:S(2)}) collective-permute-start(s32[2,4,8]{2,1,0:T(4,128)S(1)} %shard_map.57), channel_id=1, source_target_pairs={{0,2},{1,31},{2,4},{3,1},{4,6},{5,3},{6,8},{7,5},{8,10},{9,7},{10,... | collective-permute-start | bytes 776 | tf_op jit(solution)/shard_map/ppermute | solution.py:35
  10.8 0.5 %collective-permute-start.2 = (s32[2,4,8]{2,1,0:T(4,128)S(1)}, s32[2,4,8]{2,1,0:T(4,128)S(1)}, u32[]{:S(2)}, u32[]{:S(2)}) collective-permute-start(s32[2,4,8]{2,1,0:T(4,128)S(1)} %collective-permute-done.1.moved_lists), channel_id=1, source_target_pairs={{0,4},{1,29},{2,6},{3,31},{4,8},{5,1},{6,10},{7,3},{8,12},{9,5},{1... | collective-permute-start | bytes 776 | tf_op jit(solution)/shard_map/ppermute | solution.py:35
  11.3 0.2 collective-permute-done.3.asked1
  11.5 3.5 %collective-permute-done.2.asked2 = s32[2,4,8]{2,1,0:T(4,128)S(1)} collective-permute-done((s32[2,4,8]{2,1,0:T(4,128)S(1)}, s32[2,4,8]{2,1,0:T(4,128)S(1)}, u32[]{:S(2)}, u32[]{:S(2)}) %collective-permute-start.2) | collective-permute-done | bytes 288 | tf_op jit(solution)/shard_map/ppermute | solution.py:35
  15.0 0.0 collective-permute-done.6.other
  15.1 0.5 %shard_map.60 = (f32[2,3,8,480]{3,2,1,0:T(8,128)S(1)}, f32[3,3,4,480]{3,2,1,0:T(4,128)S(1)}, f32[3,4,480]{2,1,0:T(4,128)S(1)}) custom-call(s32[1]{0:T(128)S(6)} %select_n.11.me, s32[2,4,8]{2,1,0:T(4,128)S(1)} %collective-permute-done.2.asked2, s32[2,4,8]{2,1,0:T(4,128)S(1)} %collective-permute-done.3.asked1, s32[4,8]{1,0:T(4,128)S(1)} %shard_map.55.mine.lists, ...), custom_call_target="tpu_custom_call" | custom-call | tf_op jit(solution)/shard_map/pallas_call | solution.py:262
  15.5 0.1 collective-permute-start.7
  15.6 1.7 %collective-permute-start.8 = (f32[3,3,4,480]{3,2,1,0:T(4,128)S(1)}, f32[3,3,4,480]{3,2,1,0:T(4,128)S(1)}, u32[]{:S(2)}, u32[]{:S(2)}) collective-permute-start(f32[3,3,4,480]{3,2,1,0:T(4,128)S(1)} %get-tuple-element.17), channel_id=1, source_target_pairs={{0,124},{1,5},{2,126},{3,7},{4,0},{5,9},{6,2},{7,11},{8,4},{9,13},... | collective-permute-start | bytes 207368 | tf_op jit(solution)/shard_map/ppermute | solution.py:35
  17.3 8.0 %collective-permute-done.7.refs_0_ = f32[2,3,8,480]{3,2,1,0:T(8,128)S(1)} collective-permute-done((f32[2,3,8,480]{3,2,1,0:T(8,128)S(1)}, f32[2,3,8,480]{3,2,1,0:T(8,128)S(1)}, u32[]{:S(2)}, u32[]{:S(2)}) %collective-permute-start.7) | collective-permute-done | bytes 92192 | tf_op jit(solution)/shard_map/ppermute | solution.py:35
  25.3 0.0 collective-permute-start.9
  25.3 0.0 collective-permute-done.8.refs_1_
  25.3 0.5 %collective-permute-start.10 = (f32[3,3,4,480]{3,2,1,0:T(4,128)S(1)}, f32[3,3,4,480]{3,2,1,0:T(4,128)S(1)}, u32[]{:S(2)}, u32[]{:S(2)}) collective-permute-start(f32[3,3,4,480]{3,2,1,0:T(4,128)S(1)} %collective-permute-done.8.refs_1_), channel_id=1, source_target_pairs={{0,1},{1,0},{2,3},{3,2},{4,5},{5,4},{6,7},{7,6},{8,9},{9,8},{10,11... | collective-permute-start | bytes 207368 | tf_op jit(solution)/shard_map/ppermute | solution.py:35
  25.8 0.0 collective-permute-start.5
  25.8 0.5 %collective-permute-start.4 = (s32[2,4,8]{2,1,0:T(4,128)S(1)}, s32[2,4,8]{2,1,0:T(4,128)S(1)}, u32[]{:S(2)}, u32[]{:S(2)}) collective-permute-start(s32[2,4,8]{2,1,0:T(4,128)S(1)} %collective-permute-done.2.asked2), channel_id=1, source_target_pairs={{0,1},{1,0},{2,3},{3,2},{4,5},{5,4},{6,7},{7,6},{8,9},{9,8},{10,11... | collective-permute-start | bytes 776 | tf_op jit(solution)/shard_map/ppermute | solution.py:35
  26.3 1.4 %shard_map.61 = (bf16[3,512,128]{2,1,0:T(8,128)(2,1)S(1)}, bf16[3,4,192,256]{3,2,1,0:T(8,128)(2,1)S(1)}, f32[2,3,128,128]{3,2,1,0:T(8,128)S(1)}) custom-call(s32[1]{0:T(128)S(6)} %select_n.11.me, f32[3,64,480]{2,1,0:T(8,128)S(1)} %shard_map.59.own.tracers, s32[1,8]{1,0:T(1,128)} %counts_in.1, f32[2,3,64,256]{3,2,1,0:T(8,128)} %bitcast.10, s32[48,64]{1,0:T(8,128)} %bitcast.11), custom_call_target="tpu_custom_call" | custom-call | tf_op jit(solution)/shard_map/pallas_call | solution.py:262
  27.7 0.0 collective-permute-done.5.lists1
  27.7 0.0 collective-permute-done.4.lists2
  27.7 0.2 shard_map.58.picks
  27.9 0.0 collective-permute-done.10.refs_3_
  27.9 0.0 collective-permute-done.9.refs_2_
  27.9 1.7 %shard_map.62.rows.tracers = f32[3,64,512]{2,1,0:T(8,128)S(1)} custom-call(f32[2,3,8,480]{3,2,1,0:T(8,128)S(1)} %collective-permute-done.7.refs_0_, f32[3,3,4,480]{3,2,1,0:T(4,128)S(1)} %collective-permute-done.8.refs_1_, f32[2,3,8,480]{3,2,1,0:T(8,128)S(1)} %collective-permute-done.9.refs_2_, f32[3,3,4,480]{3,2,1,0:T(4,128)S(1)} %collective-permute-done.10.refs_3_, ...), custom_call_target="tpu_custom_call" | custom-call | tf_op jit(solution)/shard_map/pallas_call | solution.py:262
  29.6 0.3 shard_map.63
  29.9 0.1 collective-permute-start.11
  30.0 1.3 %collective-permute-done.11.lent = f32[3,16,512]{2,1,0:T(8,128)S(1)} collective-permute-done((f32[3,16,512]{2,1,0:T(8,128)S(1)}, f32[3,16,512]{2,1,0:T(8,128)S(1)}, u32[]{:S(2)}, u32[]{:S(2)}) %collective-permute-start.11) | collective-permute-done | bytes 98336 | tf_op jit(solution)/shard_map/ppermute | solution.py:35
  31.3 0.8 %collective-permute-start.12 = (f32[2,3,8,512]{3,2,1,0:T(8,128)S(1)}, f32[2,3,8,512]{3,2,1,0:T(8,128)S(1)}, u32[]{:S(2)}, u32[]{:S(2)}) collective-permute-start(f32[2,3,8,512]{3,2,1,0:T(8,128)S(1)} %get-tuple-element.24), channel_id=1, source_target_pairs={{0,126},{1,3},{2,0},{3,5},{4,2},{5,7},{6,4},{7,9},{8,6},{9,11},{10... | collective-permute-start | bytes 294920 | tf_op jit(solution)/shard_map/ppermute | solution.py:35
  32.1 0.2 collective-permute-start.13
  32.2 9.6 %collective-permute-done.12.refs_0_ = f32[2,3,8,512]{3,2,1,0:T(8,128)S(1)} collective-permute-done((f32[2,3,8,512]{3,2,1,0:T(8,128)S(1)}, f32[2,3,8,512]{3,2,1,0:T(8,128)S(1)}, u32[]{:S(2)}, u32[]{:S(2)}) %collective-permute-start.12) | collective-permute-done | bytes 98336 | tf_op jit(solution)/shard_map/ppermute | solution.py:35
  41.8 0.0 collective-permute-start.14
  41.8 0.0 collective-permute-done.13.refs_1_
  41.8 1.4 %collective-permute-start.15 = (f32[3,3,4,512]{3,2,1,0:T(4,128)S(1)}, f32[3,3,4,512]{3,2,1,0:T(4,128)S(1)}, u32[]{:S(2)}, u32[]{:S(2)}) collective-permute-start(f32[3,3,4,512]{3,2,1,0:T(4,128)S(1)} %collective-permute-done.13.refs_1_), channel_id=1, source_target_pairs={{0,1},{1,0},{2,3},{3,2},{4,5},{5,4},{6,7},{7,6},{8,9},{9,8},{10,11... | collective-permute-start | bytes 221192 | tf_op jit(solution)/shard_map/ppermute | solution.py:35
  43.2 0.2 shard_map.65.refs_5_
  43.4 0.7 %collective-permute-done.15.refs_3_ = f32[3,3,4,512]{3,2,1,0:T(4,128)S(1)} collective-permute-done((f32[3,3,4,512]{3,2,1,0:T(4,128)S(1)}, f32[3,3,4,512]{3,2,1,0:T(4,128)S(1)}, u32[]{:S(2)}, u32[]{:S(2)}) %collective-permute-start.15) | collective-permute-done | bytes 73760 | tf_op jit(solution)/shard_map/ppermute | solution.py:35
  44.1 0.0 collective-permute-done.14.refs_2_
  44.1 2.4 %shard_map.66 = f32[3,64,480]{2,1,0:T(8,128)} custom-call(f32[2,3,8,512]{3,2,1,0:T(8,128)S(1)} %collective-permute-done.12.refs_0_, f32[3,3,4,512]{3,2,1,0:T(4,128)S(1)} %collective-permute-done.13.refs_1_, f32[2,3,8,512]{3,2,1,0:T(8,128)S(1)} %collective-permute-done.14.refs_2_, f32[3,3,4,512]{3,2,1,0:T(4,128)S(1)} %collective-permute-done.15.refs_3_, ...), custom_call_target="tpu_custom_call" | custom-call | tf_op jit(solution)/shard_map/pallas_call | solution.py:262
  (3 shorter events, 0.0 us)
Async XLA Ops:
  0.0 15.0 %collective-permute-start.6 = (f32[3,64,480]{2,1,0:T(8,128)}, f32[3,64,480]{2,1,0:T(8,128)S(1)}, u32[]{:S(2)}, u32[]{:S(2)}) collective-permute-start(f32[3,64,480]{2,1,0:T(8,128)} %bitcast.8), channel_id=1, source_target_pairs={{0,1},{1,0},{2,3},{3,2},{4,5},{5,4},{6,7},{7,6},{8,9},{9,8},{10,11... | collective-permute-start | bytes 1105928 | tf_op jit(solution)/shard_map/ppermute | solution.py:35
  1.4 1.6 %collective-permute-start = (s32[4,8]{1,0:T(4,128)}, s32[4,8]{1,0:T(4,128)S(1)}, u32[]{:S(2)}, u32[]{:S(2)}) collective-permute-start(s32[4,8]{1,0:T(4,128)} %bitcast.12), channel_id=1, source_target_pairs={{0,1},{1,0},{2,3},{3,2},{4,5},{5,4},{6,7},{7,6},{8,9},{9,8},{10,11... | collective-permute-start | bytes 392 | tf_op jit(solution)/shard_map/ppermute | solution.py:35
  2.9 5.8 %collective-permute-start.1 = (s32[2,4,8]{2,1,0:T(4,128)S(1)}, s32[2,4,8]{2,1,0:T(4,128)S(1)}, u32[]{:S(2)}, u32[]{:S(2)}) collective-permute-start(s32[2,4,8]{2,1,0:T(4,128)S(1)} %shard_map.56.both), channel_id=1, source_target_pairs={{0,0},{1,97},{2,2},{3,99},{4,4},{5,5},{6,6},{7,7},{8,8},{9,9},{10,... | collective-permute-start | bytes 776 | tf_op jit(solution)/shard_map/ppermute | solution.py:35
  8.7 2.8 %collective-permute-start.3 = (s32[2,4,8]{2,1,0:T(4,128)S(1)}, s32[2,4,8]{2,1,0:T(4,128)S(1)}, u32[]{:S(2)}, u32[]{:S(2)}) collective-permute-start(s32[2,4,8]{2,1,0:T(4,128)S(1)} %shard_map.57), channel_id=1, source_target_pairs={{0,2},{1,31},{2,4},{3,1},{4,6},{5,3},{6,8},{7,5},{8,10},{9,7},{10,... | collective-permute-start | bytes 776 | tf_op jit(solution)/shard_map/ppermute | solution.py:35
  10.8 4.3 %collective-permute-start.2 = (s32[2,4,8]{2,1,0:T(4,128)S(1)}, s32[2,4,8]{2,1,0:T(4,128)S(1)}, u32[]{:S(2)}, u32[]{:S(2)}) collective-permute-start(s32[2,4,8]{2,1,0:T(4,128)S(1)} %collective-permute-done.1.moved_lists), channel_id=1, source_target_pairs={{0,4},{1,29},{2,6},{3,31},{4,8},{5,1},{6,10},{7,3},{8,12},{9,5},{1... | collective-permute-start | bytes 776 | tf_op jit(solution)/shard_map/ppermute | solution.py:35
  15.5 9.7 %collective-permute-start.7 = (f32[2,3,8,480]{3,2,1,0:T(8,128)S(1)}, f32[2,3,8,480]{3,2,1,0:T(8,128)S(1)}, u32[]{:S(2)}, u32[]{:S(2)}) collective-permute-start(f32[2,3,8,480]{3,2,1,0:T(8,128)S(1)} %get-tuple-element.16), channel_id=1, source_target_pairs={{0,126},{1,3},{2,0},{3,5},{4,2},{5,7},{6,4},{7,9},{8,6},{9,11},{10... | collective-permute-start | bytes 276488 | tf_op jit(solution)/shard_map/ppermute | solution.py:35
  15.6 9.7 %collective-permute-start.8 = (f32[3,3,4,480]{3,2,1,0:T(4,128)S(1)}, f32[3,3,4,480]{3,2,1,0:T(4,128)S(1)}, u32[]{:S(2)}, u32[]{:S(2)}) collective-permute-start(f32[3,3,4,480]{3,2,1,0:T(4,128)S(1)} %get-tuple-element.17), channel_id=1, source_target_pairs={{0,124},{1,5},{2,126},{3,7},{4,0},{5,9},{6,2},{7,11},{8,4},{9,13},... | collective-permute-start | bytes 207368 | tf_op jit(solution)/shard_map/ppermute | solution.py:35
  25.3 2.7 %collective-permute-start.9 = (f32[2,3,8,480]{3,2,1,0:T(8,128)S(1)}, f32[2,3,8,480]{3,2,1,0:T(8,128)S(1)}, u32[]{:S(2)}, u32[]{:S(2)}) collective-permute-start(f32[2,3,8,480]{3,2,1,0:T(8,128)S(1)} %collective-permute-done.7.refs_0_), channel_id=1, source_target_pairs={{0,1},{1,0},{2,3},{3,2},{4,5},{5,4},{6,7},{7,6},{8,9},{9,8},{10,11... | collective-permute-start | bytes 276488 | tf_op jit(solution)/shard_map/ppermute | solution.py:35
  25.3 2.6 %collective-permute-start.10 = (f32[3,3,4,480]{3,2,1,0:T(4,128)S(1)}, f32[3,3,4,480]{3,2,1,0:T(4,128)S(1)}, u32[]{:S(2)}, u32[]{:S(2)}) collective-permute-start(f32[3,3,4,480]{3,2,1,0:T(4,128)S(1)} %collective-permute-done.8.refs_1_), channel_id=1, source_target_pairs={{0,1},{1,0},{2,3},{3,2},{4,5},{5,4},{6,7},{7,6},{8,9},{9,8},{10,11... | collective-permute-start | bytes 207368 | tf_op jit(solution)/shard_map/ppermute | solution.py:35
  25.8 1.9 %collective-permute-start.5 = (s32[2,4,8]{2,1,0:T(4,128)S(1)}, s32[2,4,8]{2,1,0:T(4,128)S(1)}, u32[]{:S(2)}, u32[]{:S(2)}) collective-permute-start(s32[2,4,8]{2,1,0:T(4,128)S(1)} %collective-permute-done.3.asked1), channel_id=1, source_target_pairs={{0,1},{1,0},{2,3},{3,2},{4,5},{5,4},{6,7},{7,6},{8,9},{9,8},{10,11... | collective-permute-start | bytes 776 | tf_op jit(solution)/shard_map/ppermute | solution.py:35
  25.8 2.0 %collective-permute-start.4 = (s32[2,4,8]{2,1,0:T(4,128)S(1)}, s32[2,4,8]{2,1,0:T(4,128)S(1)}, u32[]{:S(2)}, u32[]{:S(2)}) collective-permute-start(s32[2,4,8]{2,1,0:T(4,128)S(1)} %collective-permute-done.2.asked2), channel_id=1, source_target_pairs={{0,1},{1,0},{2,3},{3,2},{4,5},{5,4},{6,7},{7,6},{8,9},{9,8},{10,11... | collective-permute-start | bytes 776 | tf_op jit(solution)/shard_map/ppermute | solution.py:35
  29.9 1.4 %collective-permute-start.11 = (f32[3,16,512]{2,1,0:T(8,128)S(1)}, f32[3,16,512]{2,1,0:T(8,128)S(1)}, u32[]{:S(2)}, u32[]{:S(2)}) collective-permute-start(f32[3,16,512]{2,1,0:T(8,128)S(1)} %get-tuple-element.23), channel_id=1, source_target_pairs={{0,1},{1,0},{2,3},{3,2},{4,5},{5,4},{6,7},{7,6},{8,9},{9,8},{10,11... | collective-permute-start | bytes 294920 | tf_op jit(solution)/shard_map/ppermute | solution.py:35
  31.3 10.5 %collective-permute-start.12 = (f32[2,3,8,512]{3,2,1,0:T(8,128)S(1)}, f32[2,3,8,512]{3,2,1,0:T(8,128)S(1)}, u32[]{:S(2)}, u32[]{:S(2)}) collective-permute-start(f32[2,3,8,512]{3,2,1,0:T(8,128)S(1)} %get-tuple-element.24), channel_id=1, source_target_pairs={{0,126},{1,3},{2,0},{3,5},{4,2},{5,7},{6,4},{7,9},{8,6},{9,11},{10... | collective-permute-start | bytes 294920 | tf_op jit(solution)/shard_map/ppermute | solution.py:35
  32.1 9.7 %collective-permute-start.13 = (f32[3,3,4,512]{3,2,1,0:T(4,128)S(1)}, f32[3,3,4,512]{3,2,1,0:T(4,128)S(1)}, u32[]{:S(2)}, u32[]{:S(2)}) collective-permute-start(f32[3,3,4,512]{3,2,1,0:T(4,128)S(1)} %get-tuple-element.25), channel_id=1, source_target_pairs={{0,124},{1,5},{2,126},{3,7},{4,0},{5,9},{6,2},{7,11},{8,4},{9,13},... | collective-permute-start | bytes 221192 | tf_op jit(solution)/shard_map/ppermute | solution.py:35
  41.8 2.3 %collective-permute-start.14 = (f32[2,3,8,512]{3,2,1,0:T(8,128)S(1)}, f32[2,3,8,512]{3,2,1,0:T(8,128)S(1)}, u32[]{:S(2)}, u32[]{:S(2)}) collective-permute-start(f32[2,3,8,512]{3,2,1,0:T(8,128)S(1)} %collective-permute-done.12.refs_0_), channel_id=1, source_target_pairs={{0,1},{1,0},{2,3},{3,2},{4,5},{5,4},{6,7},{7,6},{8,9},{9,8},{10,11... | collective-permute-start | bytes 294920 | tf_op jit(solution)/shard_map/ppermute | solution.py:35
  41.8 2.3 %collective-permute-start.15 = (f32[3,3,4,512]{3,2,1,0:T(4,128)S(1)}, f32[3,3,4,512]{3,2,1,0:T(4,128)S(1)}, u32[]{:S(2)}, u32[]{:S(2)}) collective-permute-start(f32[3,3,4,512]{3,2,1,0:T(4,128)S(1)} %collective-permute-done.13.refs_1_), channel_id=1, source_target_pairs={{0,1},{1,0},{2,3},{3,2},{4,5},{5,4},{6,7},{7,6},{8,9},{9,8},{10,11... | collective-permute-start | bytes 221192 | tf_op jit(solution)/shard_map/ppermute | solution.py:35
